TPU v7x, 128 devices: a whole 4x4x4 slice. The times are simulated.
128 devices in a mesh: px: 8 (over y, core), py: 16 (over x, z).
Axes of the slice: x: 4, y: 4, z: 4, core: 2. Of those that a mesh axis runs over, the one named last changes fastest.
Arguments:
- control_start: float32 [2, 16, 128, 2048], P(None, 'py', None, 'px'), may hold values from -12 to 12
- coef_x: float32 [16, 128, 2048], P('py', None, 'px'), may hold values from 0.1 to 0.45
- coef_y: float32 [16, 128, 2048], P('py', 'px'), may hold values from 0.1 to 0.45
- innovation: float32 [131072, 128], P(('px', 'py')), may hold values from -6 to 6
- obs_weight: float32 [131072, 128], P(('px', 'py')), may hold values from 0.25 to 4
- interp: float32 [131072], P(('px', 'py')), may hold values from 0 to 1
- obs_owner: int32 [131072, 1], P(('px', 'py')), may hold values from 0 to 15; in each aligned block of 1024 rows (0 to 1023, 1024 to 2047, ...) at most 192 rows name the same one
- cell_key: int32 [131072], P(('px', 'py')), may hold values from 0 to 31
- stencil: int32 [131072], P(('px', 'py')), may hold values from 0 to 14
Outputs:
- control: float32 [2, 16, 128, 2048], P(None, 'py', None, 'px')
- residual: float32 [2, 16, 128, 2048], P(None, 'py', None, 'px')
Inputs may be any that keep to these rules, and one draw needn't show every extreme that they name: `obs_owner`: at most 192 of the observation rows of one device name the same owner, and exactly 192 do for some owner on some device.
All inputs are finite; a program needn't handle non-finite values.
Results may differ from a plain program's by a relative error of at most 0.00023.
Values sent between devices are 32-bit elements; how exact they have to be, the bound alone decides.
A program may use at most 64 MiB of HBM per device.

v0:
```python
import jax
import jax.numpy as jnp
from jax import lax
from jax.sharding import PartitionSpec as P

F = 2
SEG = 128
M = 4
ITERS = 2
LZ = 1
LX = 16
NB = 16


def diffuse(values, coeffs, axis_dim):
    length = values.shape[axis_dim]
    face_coef = lax.slice_in_dim(coeffs[None], 0, length - 1, axis=axis_dim)
    pad_after = [(0, 0)] * values.ndim
    pad_before = [(0, 0)] * values.ndim
    pad_after[axis_dim] = (0, 1)
    pad_before[axis_dim] = (1, 0)
    for repeat in range(M):
        next_cell = lax.slice_in_dim(values, 1, length, axis=axis_dim)
        this_cell = lax.slice_in_dim(values, 0, length - 1, axis=axis_dim)
        flux_face = face_coef * (next_cell - this_cell)
        values = values + jnp.pad(flux_face, pad_after) - jnp.pad(flux_face, pad_before)
    return values


def build_interp(shares_in, rows_in, row_count):
    row_ids = jnp.arange(row_count, dtype=jnp.int32)[None, :]
    lower_hit = (rows_in[:, None] == row_ids).astype(jnp.float32)
    upper_hit = (rows_in[:, None] + NB == row_ids).astype(jnp.float32)
    shares = shares_in[:, None]
    return (1.0 - shares) * lower_hit + shares * upper_hit


def misfit(state_in, observed, weights, interp_matrix):
    flat_field = state_in.reshape(-1, SEG)
    modelled = jnp.dot(
        interp_matrix,
        flat_field,
        precision=lax.Precision.HIGHEST,
        preferred_element_type=jnp.float32,
    )
    weighted = weights * (observed - modelled)
    result = lax.dot_general(
        interp_matrix,
        weighted,
        (((0,), (0,)), ((), ())),
        precision=lax.Precision.HIGHEST,
        preferred_element_type=jnp.float32,
    )
    return result.reshape(state_in.shape)


def dot_total(left_side, right_side):
    return lax.psum(jnp.sum(left_side * right_side), ("px", "py"))


def shards(
    control_start, coef_x, coef_y, innovation, obs_weight, interp, obs_owner, cell_key, stencil
):
    groups = lax.axis_size("py")
    capacity = 3 * innovation.shape[0] // groups
    coef_x = coef_x.at[:, -1, :].set(0.0)
    coef_y = coef_y.at[:, :, -1].set(0.0)
    field_id = cell_key // (LZ * NB)
    level_local = cell_key // NB % LZ
    row_index = ((field_id * LZ + level_local) * LX + stencil) * NB + cell_key % NB
    targets = obs_owner[:, 0]
    onehot = (targets[:, None] == jnp.arange(groups, dtype=jnp.int32)[None, :]).astype(jnp.int32)
    earlier = jnp.cumsum(onehot, axis=0) - onehot
    slot_index = jnp.sum(earlier * onehot, axis=1)
    slot_target = targets * capacity + slot_index
    total_slots = groups * capacity

    def bucket(values_in):
        buf_shape = (total_slots,) + values_in.shape[1:]
        return jnp.zeros(buf_shape, values_in.dtype).at[slot_target].set(values_in)

    arrived = (
        lax.all_to_all(bucket(innovation), "py", split_axis=0, concat_axis=0, tiled=True),
        lax.all_to_all(bucket(obs_weight), "py", split_axis=0, concat_axis=0, tiled=True),
        lax.all_to_all(bucket(interp), "py", split_axis=0, concat_axis=0, tiled=True),
        lax.all_to_all(bucket(row_index), "py", split_axis=0, concat_axis=0, tiled=True),
    )
    observed, weights, shares_in, rows_in = arrived
    interp_matrix = build_interp(shares_in, rows_in, F * LZ * LX * NB)

    def forward(values_in):
        turned = lax.all_to_all(
            diffuse(values_in, coef_x, 2), "px", split_axis=2, concat_axis=3, tiled=True
        )
        return diffuse(turned, coef_y, 3)

    def adjoint(values_in):
        turned = lax.all_to_all(
            diffuse(values_in, coef_y, 3), "px", split_axis=3, concat_axis=2, tiled=True
        )
        return diffuse(turned, coef_x, 2)

    no_data = jnp.zeros_like(observed)
    residual = (
        adjoint(misfit(forward(control_start), observed, weights, interp_matrix)) - control_start
    )
    control = control_start
    direction = residual
    norm_now = dot_total(residual, residual)
    for repeat in range(ITERS):
        applied = direction - adjoint(misfit(forward(direction), no_data, weights, interp_matrix))
        step_size = norm_now / dot_total(direction, applied)
        control = control + step_size * direction
        residual = residual - step_size * applied
        norm_next = dot_total(residual, residual)
        direction = residual + norm_next / norm_now * direction
        norm_now = norm_next
    return (control, residual)


def solution(mesh):
    return jax.shard_map(
        shards,
        mesh=mesh,
        in_specs=(
            P(None, "py", None, "px"),
            P("py", None, "px"),
            P("py", "px", None),
            P(("px", "py"), None),
            P(("px", "py"), None),
            P(("px", "py")),
            P(("px", "py"), None),
            P(("px", "py")),
            P(("px", "py")),
        ),
        out_specs=(P(None, "py", None, "px"), P(None, "py", None, "px")),
        check_vma=False,
    )
```

profile of v0, /device:TPU:1, one launch (start us, length us, event | category | flops | bytes accessed | tf_op | source)
XLA Modules:
  0.0 462.8 jit_solution(5884328285071608332)
XLA Ops:
  1.4 4.5 reduce-window.6
  8.4 4.3 scatter_custom_fusion
  13.5 8.4 %all-to-all-start = ((s32[16,192,1]{1,2,0:T(1,128)}), s32[16,192,1]{1,2,0:T(1,128)S(1)}, u32[]{:S(2)}, u32[]{:S(2)}) async-start(s32[16,192,1]{1,2,0:T(1,128)} %all_to_all.143), calls=%async_computation | async-start | bytes 32768 | tf_op jit(solution)/shard_map/all_to_all | solution.py:86
  24.9 4.5 scatter_custom_fusion.1
  30.0 6.7 %all-to-all-start.1 = ((f32[16,192,1]{1,2,0:T(1,128)}), f32[16,192,1]{1,2,0:T(1,128)S(1)}, u32[]{:S(2)}, u32[]{:S(2)}) async-start(f32[16,192,1]{1,2,0:T(1,128)} %all_to_all.144), calls=%async_computation.1 | async-start | bytes 32768 | tf_op jit(solution)/shard_map/all_to_all | solution.py:85
  36.8 4.7 %scatter_custom_fusion.2 = f32[3072,128]{1,0:T(8,128)} fusion(s32[1024]{0:T(1024)S(1)} %bitcast.132, f32[1024,128]{1,0:T(8,128)} %param.17, f32[]{:T(128)} %constant.119.clone.1), kind=kCustom, calls=%fused_computation.51 | custom fusion | bytes 1573376 | tf_op jit(solution)/shard_map/scatter | solution.py:80
  41.5 4.7 %scatter_custom_fusion.3 = f32[3072,128]{1,0:T(8,128)} fusion(s32[1024]{0:T(1024)S(1)} %bitcast.133, f32[1024,128]{1,0:T(8,128)} %param.16, f32[]{:T(128)} %constant.119.clone.1), kind=kCustom, calls=%fused_computation.49 | custom fusion | bytes 1573376 | tf_op jit(solution)/shard_map/scatter | solution.py:80
  47.2 6.0 %all-to-all-start.4 = ((f32[2,1,128,256]{3,0,1,2:T(2,128)}), f32[2,1,128,256]{3,0,1,2:T(2,128)S(1)}, u32[]{:S(2)}, u32[]{:S(2)}) async-start(f32[2,1,128,256]{3,0,1,2:T(2,128)} %copy.120), calls=%async_computation.4 | async-start | bytes 524288 | tf_op jit(solution)/shard_map/all_to_all | solution.py:92
  53.3 6.4 %all-to-all-done.4 = f32[2,1,128,256]{3,0,1,2:T(2,128)S(1)} async-done(((f32[2,1,128,256]{3,0,1,2:T(2,128)}), f32[2,1,128,256]{3,0,1,2:T(2,128)S(1)}, u32[]{:S(2)}, u32[]{:S(2)}) %all-to-all-start.4) | async-done | bytes 262176 | tf_op jit(solution)/shard_map/all_to_all | solution.py:92
  59.6 6.9 %all-to-all-start.2 = ((f32[16,192,128]{2,1,0:T(8,128)}), f32[16,192,128]{2,1,0:T(8,128)S(1)}, u32[]{:S(2)}, u32[]{:S(2)}) async-start(f32[16,192,128]{2,1,0:T(8,128)} %bitcast.7), calls=%async_computation.2 | async-start | bytes 3145728 | tf_op jit(solution)/shard_map/all_to_all | solution.py:84
  67.2 19.9 %all-to-all-done.2 = f32[16,192,128]{2,1,0:T(8,128)S(1)} async-done(((f32[16,192,128]{2,1,0:T(8,128)}), f32[16,192,128]{2,1,0:T(8,128)S(1)}, u32[]{:S(2)}, u32[]{:S(2)}) %all-to-all-start.2) | async-done | bytes 1572896 | tf_op jit(solution)/shard_map/all_to_all | solution.py:84
  87.1 4.7 %all-to-all-start.3 = ((f32[16,192,128]{2,1,0:T(8,128)}), f32[16,192,128]{2,1,0:T(8,128)}, u32[]{:S(2)}, u32[]{:S(2)}) async-start(f32[16,192,128]{2,1,0:T(8,128)} %bitcast.9), calls=%async_computation.3 | async-start | bytes 3145728 | tf_op jit(solution)/shard_map/all_to_all | solution.py:83
  92.4 18.5 %all-to-all-done.3 = f32[16,192,128]{2,1,0:T(8,128)} async-done(((f32[16,192,128]{2,1,0:T(8,128)}), f32[16,192,128]{2,1,0:T(8,128)}, u32[]{:S(2)}, u32[]{:S(2)}) %all-to-all-start.3) | async-done | bytes 1572896 | tf_op jit(solution)/shard_map/all_to_all | solution.py:83
  111.0 9.3 %fusion.11 = f32[3072,128]{1,0:T(8,128)S(1)} fusion(f32[3072,128]{1,0:T(8,128)S(1)} %bitcast.117, f32[3072,128]{1,0:T(8,128)} %bitcast.10, f32[512,128]{1,0:T(8,128)S(1)} %reshape.123, f32[3072]{0:T(1024)S(1)} %all_to_all.112, s32[3072]{0:T(1024)S(1)} %broadcast_add_fusion.1, f32[3072]{0:T(1024)S(1)} %broadcast_subtract_fusion, s32[3072]{0:T(1024)S(1)} %eq.64), kind=kOutput, calls=%fused_computation.18 | convolution fusion | flops 2424569856 | bytes 5029888 | tf_op jit(solution)/shard_map/dot_general | solution.py:40
  120.2 11.8 %fusion.4 = f32[512,128]{1,0:T(8,128)S(1)} fusion(f32[3072,128]{1,0:T(8,128)S(1)} %fusion.11, f32[3072]{0:T(1024)S(1)} %all_to_all.112, s32[3072]{0:T(1024)S(1)} %broadcast_add_fusion.1, f32[3072]{0:T(1024)S(1)} %broadcast_subtract_fusion, s32[3072]{0:T(1024)S(1)} %eq.64), kind=kOutput, calls=%fused_computation.10 | convolution fusion | flops 2423783424 | bytes 1884160 | tf_op jit(solution)/shard_map/dot_general | solution.py:47
  134.4 2.9 reshape.171
  137.3 14.4 %all_to_all.155 = f32[8,1,8192]{2,1,0:T(1,128)S(1)} all-to-all(f32[8,1,8192]{2,1,0:T(1,128)S(1)} %reshape.171), channel_id=1, replica_groups=mesh['px'=8,'py'=16] {'px'}, dimensions={0} | all-to-all | bytes 524288 | tf_op jit(solution)/shard_map/all_to_all | solution.py:98
  153.5 2.8 reshape.172
  158.1 9.9 %all_to_all.156 = f32[2,1,128,256]{3,0,1,2:T(2,128)S(1)} all-to-all(f32[2,1,128,256]{3,0,1,2:T(2,128)S(1)} %copy.127), channel_id=1, replica_groups=mesh['px'=8,'py'=16] {'px'}, dimensions={2} | all-to-all | bytes 524288 | tf_op jit(solution)/shard_map/all_to_all | solution.py:92
  170.1 9.3 %fusion.10 = f32[3072,128]{1,0:T(8,128)S(1)} fusion(f32[3072,128]{1,0:T(8,128)S(1)} %bitcast.118, f32[512,128]{1,0:T(8,128)S(1)} %reshape.125, f32[3072]{0:T(1024)S(1)} %all_to_all.112, s32[3072]{0:T(1024)S(1)} %broadcast_add_fusion.1, f32[3072]{0:T(1024)S(1)} %broadcast_subtract_fusion, s32[3072]{0:T(1024)S(1)} %eq.64), kind=kOutput, calls=%fused_computation.17 | convolution fusion | flops 2424569856 | bytes 3457024 | tf_op jit(solution)/shard_map/dot_general | solution.py:40
  179.4 11.8 %fusion.2 = f32[512,128]{1,0:T(8,128)S(1)} fusion(f32[3072,128]{1,0:T(8,128)S(1)} %fusion.10, f32[3072]{0:T(1024)S(1)} %all_to_all.112, s32[3072]{0:T(1024)S(1)} %broadcast_add_fusion.1, f32[3072]{0:T(1024)S(1)} %broadcast_subtract_fusion, s32[3072]{0:T(1024)S(1)} %eq.64), kind=kOutput, calls=%fused_computation.8 | convolution fusion | flops 2423783424 | bytes 1884160 | tf_op jit(solution)/shard_map/dot_general | solution.py:47
  193.6 2.9 reshape.173
  196.5 9.9 %all_to_all.157 = f32[8,1,8192]{2,1,0:T(1,128)S(1)} all-to-all(f32[8,1,8192]{2,1,0:T(1,128)S(1)} %reshape.173), channel_id=1, replica_groups=mesh['px'=8,'py'=16] {'px'}, dimensions={0} | all-to-all | bytes 524288 | tf_op jit(solution)/shard_map/all_to_all | solution.py:98
  207.7 2.8 reshape.174
  212.4 63.0 %all-reduce.96 = (f32[]{:T(128)}, f32[]{:T(128)}) all-reduce(f32[]{:T(128)} %get-tuple-element.35, f32[]{:T(128)} %get-tuple-element.34), channel_id=1, replica_groups=mesh['px'=8,'py'=16] {'px','py'}, use_global_device_ids=true, to_apply=%region_8.9 | all-reduce | flops 2 | bytes 16 | tf_op jit(solution)/shard_map/psum | solution.py:58
  277.4 62.5 %psum.30 = f32[]{:T(128)} all-reduce(f32[]{:T(128)} %get-tuple-element.38), channel_id=1, replica_groups=mesh['px'=8,'py'=16] {'px','py'}, use_global_device_ids=true, to_apply=%region_12.13 | all-reduce | flops 1 | bytes 8 | tf_op jit(solution)/shard_map/psum | solution.py:58
  341.8 11.0 %all_to_all.158 = f32[2,1,128,256]{3,0,1,2:T(2,128)S(1)} all-to-all(f32[2,1,128,256]{3,0,1,2:T(2,128)S(1)} %copy.134), channel_id=1, replica_groups=mesh['px'=8,'py'=16] {'px'}, dimensions={2} | all-to-all | bytes 524288 | tf_op jit(solution)/shard_map/all_to_all | solution.py:92
  354.8 9.1 %fusion.9 = f32[3072,128]{1,0:T(8,128)S(1)} fusion(f32[3072,128]{1,0:T(8,128)S(1)} %bitcast.119, f32[512,128]{1,0:T(8,128)S(1)} %reshape.127, f32[3072]{0:T(1024)S(1)} %all_to_all.112, s32[3072]{0:T(1024)S(1)} %broadcast_add_fusion.1, f32[3072]{0:T(1024)S(1)} %broadcast_subtract_fusion, s32[3072]{0:T(1024)S(1)} %eq.64), kind=kOutput, calls=%fused_computation.16 | convolution fusion | flops 2424569856 | bytes 3457024 | tf_op jit(solution)/shard_map/dot_general | solution.py:40
  364.0 11.8 %fusion = f32[512,128]{1,0:T(8,128)S(1)} fusion(f32[3072,128]{1,0:T(8,128)S(1)} %fusion.9, f32[3072]{0:T(1024)S(1)} %all_to_all.112, s32[3072]{0:T(1024)S(1)} %broadcast_add_fusion.1, f32[3072]{0:T(1024)S(1)} %broadcast_subtract_fusion, s32[3072]{0:T(1024)S(1)} %eq.64), kind=kOutput, calls=%fused_computation.6 | convolution fusion | flops 2423783424 | bytes 1884160 | tf_op jit(solution)/shard_map/dot_general | solution.py:47
  378.2 2.9 reshape.175
  381.1 9.9 %all_to_all.159 = f32[8,1,8192]{2,1,0:T(1,128)S(1)} all-to-all(f32[8,1,8192]{2,1,0:T(1,128)S(1)} %reshape.175), channel_id=1, replica_groups=mesh['px'=8,'py'=16] {'px'}, dimensions={0} | all-to-all | bytes 524288 | tf_op jit(solution)/shard_map/all_to_all | solution.py:98
  397.0 63.1 %psum.31 = f32[]{:T(128)} all-reduce(f32[]{:T(128)} %multiply_reduce_fusion), channel_id=1, replica_groups=mesh['px'=8,'py'=16] {'px','py'}, use_global_device_ids=true, to_apply=%region_14.15 | all-reduce | flops 1 | bytes 8 | tf_op jit(solution)/shard_map/psum | solution.py:58
  (161 shorter events, 35.5 us)
Async XLA Ops:
  0.6 23.3 %copy-start = (f32[2,1,128,256]{3,2,1,0:T(8,128)S(1)}, f32[2,1,128,256]{3,2,1,0:T(8,128)}, u32[]{:S(2)}) copy-start(f32[2,1,128,256]{3,2,1,0:T(8,128)} %param.13) | copy-start | bytes 786436
  13.5 16.6 %all-to-all-start = ((s32[16,192,1]{1,2,0:T(1,128)}), s32[16,192,1]{1,2,0:T(1,128)S(1)}, u32[]{:S(2)}, u32[]{:S(2)}) async-start(s32[16,192,1]{1,2,0:T(1,128)} %all_to_all.143), calls=%async_computation | async-start | bytes 32768 | tf_op jit(solution)/shard_map/all_to_all | solution.py:86
  23.9 0.9 copy-start.6
  30.0 17.1 %all-to-all-start.1 = ((f32[16,192,1]{1,2,0:T(1,128)}), f32[16,192,1]{1,2,0:T(1,128)S(1)}, u32[]{:S(2)}, u32[]{:S(2)}) async-start(f32[16,192,1]{1,2,0:T(1,128)} %all_to_all.144), calls=%async_computation.1 | async-start | bytes 32768 | tf_op jit(solution)/shard_map/all_to_all | solution.py:85
  47.2 12.5 %all-to-all-start.4 = ((f32[2,1,128,256]{3,0,1,2:T(2,128)}), f32[2,1,128,256]{3,0,1,2:T(2,128)S(1)}, u32[]{:S(2)}, u32[]{:S(2)}) async-start(f32[2,1,128,256]{3,0,1,2:T(2,128)} %copy.120), calls=%async_computation.4 | async-start | bytes 524288 | tf_op jit(solution)/shard_map/all_to_all | solution.py:92
  59.6 27.5 %all-to-all-start.2 = ((f32[16,192,128]{2,1,0:T(8,128)}), f32[16,192,128]{2,1,0:T(8,128)S(1)}, u32[]{:S(2)}, u32[]{:S(2)}) async-start(f32[16,192,128]{2,1,0:T(8,128)} %bitcast.7), calls=%async_computation.2 | async-start | bytes 3145728 | tf_op jit(solution)/shard_map/all_to_all | solution.py:84
  87.1 23.8 %copy-start.3 = (f32[16,192,128]{2,1,0:T(8,128)}, f32[16,192,128]{2,1,0:T(8,128)S(1)}, u32[]{:S(2)}) copy-start(f32[16,192,128]{2,1,0:T(8,128)S(1)} %all-to-all-done.2) | copy-start | bytes 4718596
  87.1 23.8 %all-to-all-start.3 = ((f32[16,192,128]{2,1,0:T(8,128)}), f32[16,192,128]{2,1,0:T(8,128)}, u32[]{:S(2)}, u32[]{:S(2)}) async-start(f32[16,192,128]{2,1,0:T(8,128)} %bitcast.9), calls=%async_computation.3 | async-start | bytes 3145728 | tf_op jit(solution)/shard_map/all_to_all | solution.py:83
  168.7 1.4 copy-start.4
  277.4 63.8 %copy-start.1 = (f32[2,1,128,256]{3,2,0,1:T(8,128)}, f32[2,1,128,256]{3,2,0,1:T(8,128)S(1)}, u32[]{:S(2)}) copy-start(f32[2,1,128,256]{3,2,0,1:T(8,128)S(1)} %get-tuple-element.39) | copy-start | bytes 786436
  353.4 1.4 copy-start.5
  396.1 65.3 %copy-start.2 = (f32[2,1,128,256]{3,2,0,1:T(8,128)S(1)}, f32[2,1,128,256]{3,2,0,1:T(8,128)}, u32[]{:S(2)}) copy-start(f32[2,1,128,256]{3,2,0,1:T(8,128)} %copy-done.1) | copy-start | bytes 786436
where the time goes:
time: 471 us; the launch traced here: 463 us
  blocking collectives  244 us (52%)
  matrix products  63.1 us (13%)
  local copies, waits for them, and re-layouts  47.9 us (10%)
  waiting for transfers between devices  44.8 us (10%)
  starting transfers between devices  32.7 us (7%)
  other arithmetic  24.4 us (5%)
  between operations  6.03 us (1%)
    psum x3, blocking collectives, dot_total(): return lax.psum(jnp.sum(left_side * right_side), ('px', 'py'))  189 us
    dot_general x3, matrix products, misfit(): lax.dot_general(interp_matrix, weighted, (((0,), (0,)), ((), ())), precis...  35.4 us
    all_to_all x3, blocking collectives, adjoint(): lax.all_to_all(diffuse(values_in, coef_y, 3), 'px', split_axis=3, concat_...  34.3 us
    dot_general x3, matrix products, misfit(): jnp.dot(interp_matrix, flat_field, precision=lax.Precision.HIGHEST, prefe...  27.7 us
    all_to_all x2, blocking collectives, forward(): lax.all_to_all(diffuse(values_in, coef_x, 2), 'px', split_axis=2, concat_...  20.9 us
    all_to_all x1, waiting for transfers between devices, shards(): lax.all_to_all(bucket(obs_weight), 'py', split_axis=0, concat_axis=0, til...  19.9 us
    unnamed x20, local copies, waits for them, and re-layouts  19.2 us
    all_to_all x1, waiting for transfers between devices, shards(): lax.all_to_all(bucket(innovation), 'py', split_axis=0, concat_axis=0, til...  18.5 us
  transfers between devices with their start and end apart: 5, of which 3 were waited for; matrix products, arithmetic and copies ran while one was open for 4% of the time, Pallas kernels for 0%

commit v1 on v0

v1 whole, which is shorter than its diff:
```python
import jax
import jax.numpy as jnp
from jax import lax
from jax.experimental import pallas as pl
from jax.experimental.pallas import tpu as pltpu
from jax.sharding import PartitionSpec as P

NPX = 8
NPY = 16
CAP = 192
ROWS = 1024
L = 128
M = 4
NB = 16
T = 512
f32 = jnp.float32
bf16 = jnp.bfloat16
MESH = pl.DeviceIdType.MESH
NT = (((1,), (1,)), ((), ()))
TN = (((0,), (0,)), ((), ()))


def dot(a, b):
    return jnp.dot(a, b, preferred_element_type=f32)


def iota(shape, axis):
    return lax.broadcasted_iota(jnp.int32, shape, axis)


def split(v):
    hi = v.astype(bf16)
    return hi, (v - hi.astype(f32)).astype(bf16)


def xsweep(v, c):
    for _ in range(M):
        flux = c * (pltpu.roll(v, L - 1, 0) - v)
        v = v + flux - pltpu.roll(flux, 1, 0)
    return v


def ysweep(v, c, last, first):
    for _ in range(M):
        r = [pltpu.roll(t, L - 1, 1) for t in v]
        flux = [c[j] * (jnp.where(last, r[(j + 1) % 3], r[j]) - v[j]) for j in range(3)]
        r = [pltpu.roll(t, 1, 1) for t in flux]
        v = [v[j] + flux[j] - jnp.where(first, r[(j + 2) % 3], r[j]) for j in range(3)]
    return v


def tri(u, d, e):
    eu = e * u
    return d * u + e * pltpu.roll(u, u.shape[0] - 1, 0) + pltpu.roll(eu, 1, 0)


def kernel(
    own, key, sten, itp, inn, wgt, cin, cxin, cyin, ctl, res,
    keys, vals, metaq, pbuf, sw, sd, sm, rw, rd, rm, rhs, tid, acc,
    tfield, tsend, bfield, bsend, cyfield, cysend, cc, halo, text, bext, cyx,
    ubuf, gbuf, abuf, rbuf, qbuf, dots, red1, red2,
    s_m, s_w, s_d, r_m, r_w, r_d, s_t, r_t, s_b, r_b, s_c, r_c, s_h, r_h, s_1, r_1, s_2, r_2,
):
    px = lax.axis_index("px")
    py = lax.axis_index("py")

    def ypeer(k):
        return lax.rem(px + k, NPX)

    def opeer(k):
        x = lax.rem(py // 4 + k // 4, 4)
        z = lax.rem(lax.rem(py, 4) + lax.rem(k, 4), 4)
        return x * 4 + z

    barrier = pltpu.get_barrier_semaphore()

    def greet_px(k, carry):
        pl.semaphore_signal(barrier, inc=1, device_id={"px": ypeer(k)}, device_id_type=MESH)
        return carry

    def greet_py(k, carry):
        pl.semaphore_signal(barrier, inc=1, device_id={"py": opeer(k)}, device_id_type=MESH)
        return carry

    lax.fori_loop(1, NPX, greet_px, 0)
    lax.fori_loop(1, NPY, greet_py, 0)

    row = iota((L, L), 0)
    col = iota((L, L), 1)
    owner = own[...]
    hit = jnp.concatenate([(owner == d).astype(f32) for d in range(NPY)], axis=0)
    hit16 = hit.astype(bf16)
    upper = (row < col).astype(f32).astype(bf16)
    before = ((row // 8 == col // 8) & (col < row)).astype(f32).astype(bf16)
    inside = dot(hit16, upper)
    count = dot(hit16, jnp.ones((L, L), bf16))
    keys[...] = jnp.where(hit > 0.5, inside + dot(before, count.astype(bf16)), -1.0)

    share = itp[...]
    s_hi, rest = split(share)
    s_hi = s_hi.astype(f32)
    rest = share - s_hi
    s_mid = rest.astype(bf16).astype(f32)
    s_lo = rest - s_mid
    cell = key[...]
    fx = ((cell // NB) * 16 + sten[...]).astype(f32)
    seg = lax.rem(cell, NB).astype(f32)
    zero = jnp.zeros((3, L), f32)
    for bl in range(8):
        pick = [t[bl:bl + 1, :] for t in (s_hi, s_mid, s_lo, fx, seg)] + [zero]
        metaq[:, bl * L:(bl + 1) * L] = jnp.concatenate(pick, axis=0).astype(bf16)

    def cut(i, carry):
        rows = pl.ds(pl.multiple_of(i * L, L), L)
        w = wgt[rows, :]
        hi, lo = split(w)
        vals[rows, 0:L] = hi
        vals[rows, L:2 * L] = lo
        hi, lo = split(w * inn[rows, :])
        vals[rows, 2 * L:3 * L] = hi
        vals[rows, 3 * L:4 * L] = lo
        return carry

    lax.fori_loop(0, 8, cut, 0)

    rowmask = iota((L, L), 0) < L - 1
    for j in range(2):
        for f in range(2):
            cc[j, f] = cin[f, :, j * L:(j + 1) * L]
        cc[j, 2] = jnp.where(rowmask, cxin[:, j * L:(j + 1) * L], 0.0)
    lanes16 = iota((16, L), 1)
    for b in range(NB):
        tile = cyin[:, b * L:(b + 1) * L]
        if b == NB - 1:
            tile = jnp.where(lanes16 < L - 1, tile, 0.0)
        cyfield[0, b, 0] = tile

    def pack(field, out):
        def one(p, carry):
            out[p, :, 0] = field[:, 2 * p]
            out[p, :, 1] = field[:, 2 * p + 1]
            right = field[:, lax.rem(2 * p + 2, NB)]
            left = field[:, lax.rem(2 * p + NB - 1, NB)]
            out[p, :, 2] = jnp.where(iota(right.shape, right.ndim - 1) < 64, right, left)
            return carry

        lax.fori_loop(0, NPX, one, 0)

    def block(ext, k):
        return ext.at[:, :, :, pl.ds(pl.multiple_of(k * 16, 16), 16), :]

    def turn(send, ext, k, ssem, rsem):
        return pltpu.make_async_remote_copy(
            src_ref=send.at[ypeer(k)], dst_ref=block(ext, px),
            send_sem=ssem.at[k], recv_sem=rsem.at[k],
            device_id={"px": ypeer(k)}, device_id_type=MESH,
        )

    def turned(send, ext, k, ssem, rsem):
        source = lax.rem(px + NPX - k, NPX)
        return pltpu.make_async_remote_copy(
            src_ref=send.at[source], dst_ref=block(ext, source),
            send_sem=ssem.at[k], recv_sem=rsem.at[k],
            device_id={"px": ypeer(k)}, device_id_type=MESH,
        )

    def start_turn(send, ext, ssem, rsem):
        def one(k, carry):
            turn(send, ext, k, ssem, rsem).start()
            return carry

        lax.fori_loop(1, NPX, one, 0)
        ext[:, :, :, pl.ds(pl.multiple_of(px * 16, 16), 16), :] = send[px]

    def end_turn(send, ext, ssem, rsem):
        def one(k, carry):
            turned(send, ext, k, ssem, rsem).wait_recv()
            turn(send, ext, k, ssem, rsem).wait_send()
            return carry

        lax.fori_loop(1, NPX, one, 0)

    pack(cyfield, cysend)

    pl.semaphore_wait(barrier, NPX - 1 + NPY - 1)

    def edge(side):
        peer = ypeer(1 if side == 1 else NPX - 1)
        return pltpu.make_async_remote_copy(
            src_ref=cc.at[side], dst_ref=halo.at[side],
            send_sem=s_h.at[side], recv_sem=r_h.at[side],
            device_id={"px": peer}, device_id_type=MESH,
        )

    edge(0).start()
    edge(1).start()
    start_turn(cysend, cyx, s_c, r_c)

    def route(buf, land, k, ssem, rsem):
        return pltpu.make_async_remote_copy(
            src_ref=buf.at[k], dst_ref=land.at[k],
            send_sem=ssem.at[k], recv_sem=rsem.at[k],
            device_id={"py": opeer(k)}, device_id_type=MESH,
        )

    slot = iota((CAP, L), 0).astype(f32)

    def gather(k):
        base = pl.multiple_of(opeer(k) * 8, 8)
        mine = keys[pl.ds(base, 8), :]
        for bl in range(8):
            pbuf[:, bl * L:(bl + 1) * L] = (slot == mine[bl:bl + 1, :]).astype(f32).astype(bf16)
        meta = lax.dot_general(metaq[...], pbuf[...], NT, preferred_element_type=f32)
        out = dot(pbuf[...], vals[...])
        return meta, out[:, 0:L] + out[:, L:2 * L], out[:, 2 * L:3 * L] + out[:, 3 * L:4 * L]

    def send_rows(k, carry):
        meta, w, wd = gather(k)
        sm[k] = meta
        sw[k] = w
        sd[k] = wd
        route(sm, rm, k, s_m, r_m).start()
        route(sw, rw, k, s_w, r_w).start()
        return carry

    lax.fori_loop(1, NPY, send_rows, 0)

    def send_data(k, carry):
        route(sd, rd, k, s_d, r_d).start()
        return carry

    lax.fori_loop(1, NPY, send_data, 0)
    meta, w, wd = gather(0)
    rm[0] = meta
    rw[0] = w
    rd[0] = wd

    for side in range(2):
        edge(side).wait_recv()
    lanes = iota((L, L), 1)
    for f in range(3):
        cc[2, f] = jnp.where(lanes < 64, halo[0, f], halo[1, f])
    end_turn(cysend, cyx, s_c, r_c)

    last = iota((16, L), 1) == L - 1
    first = iota((16, L), 1) == 0

    def tiles(count, body):
        def one(t, carry):
            body(t // 2, lax.rem(t, 2))
            return carry

        lax.fori_loop(0, count, one, 0)

    def chunks(body):
        def one(i, carry):
            rows = pl.ds(pl.multiple_of(i * 16, 16), 16)
            c = [cyx[0, j, 0, rows, :] for j in range(3)]
            for f in range(2):
                body(f, rows, c)
            return carry

        lax.fori_loop(0, 8, one, 0)

    def first_x(j, f):
        ubuf[j, f] = xsweep(cc[j, f], cc[j, 2])

    def first_y(f, rows, c):
        v = ysweep([ubuf[j, f, rows, :] for j in range(3)], c, last, first)
        for j in range(3):
            ubuf[j, f, rows, :] = v[j]

    tiles(6, first_x)
    chunks(first_y)

    pick = jnp.where(iota((8, L), 0) < 3, 1.0, 0.0).astype(bf16)
    target = iota((T, 4 * CAP), 0).astype(f32)

    def group(g, land, buf, ssem, rsem, with_meta, parts):
        for i in range(4):
            k = 4 * g + i

            @pl.when(k > 0)
            def _():
                if with_meta:
                    route(sm, rm, k, s_m, r_m).wait_recv()
                route(buf, land, k, ssem, rsem).wait_recv()

            meta = rm[k]
            s = lax.dot_general(meta.astype(bf16), pick, TN, preferred_element_type=f32)
            v = land[k]
            va = v * (1.0 - s)
            vs = v * s
            terms = (va * (1.0 - s), vs * s, vs * (1.0 - s)) if parts == 3 else (va, vs)
            rows = slice(i * CAP, (i + 1) * CAP)
            for n, term in enumerate(terms):
                hi, lo = split(term)
                rhs[rows, 2 * n * L:(2 * n + 1) * L] = hi
                rhs[rows, (2 * n + 1) * L:(2 * n + 2) * L] = lo
            tid[0:1, rows] = meta[4:5, :] * 32.0 + meta[3:4, :]
        onehot = (target == tid[0:1, :]).astype(f32).astype(bf16)
        width = 2 * parts * L
        part = dot(onehot, rhs[:, 0:width])

        @pl.when(g == 0)
        def _():
            acc[:, 0:width] = part

        @pl.when(g > 0)
        def _():
            acc[:, 0:width] += part

    def w_group(g, carry):
        group(g, rw, sw, s_w, r_w, True, 3)
        return carry

    lax.fori_loop(0, 4, w_group, 0)

    def column(n):
        return acc[:, 2 * n * L:(2 * n + 1) * L] + acc[:, (2 * n + 1) * L:(2 * n + 2) * L]

    tfield[0] = (column(0) + pltpu.roll(column(1), 1, 0)).reshape(NB, 2, 16, L)
    tfield[1] = column(2).reshape(NB, 2, 16, L)
    pack(tfield, tsend)
    start_turn(tsend, text, s_t, r_t)
    end_turn(tsend, text, s_t, r_t)

    def mid_chunk(f, rows, c):
        u = [ubuf[j, f, rows, :] for j in range(3)]
        v = [tri(u[j], text[0, j, f, rows, :], text[1, j, f, rows, :]) for j in range(3)]
        v = ysweep(v, c, last, first)
        for j in range(3):
            gbuf[j, f, rows, :] = v[j]

    chunks(mid_chunk)

    def image_start(j, f):
        abuf[j, f] = cc[j, f] + xsweep(gbuf[j, f], cc[j, 2])

    tiles(6, image_start)

    def d_group(g, carry):
        group(g, rd, sd, s_d, r_d, False, 2)
        return carry

    lax.fori_loop(0, 4, d_group, 0)
    bfield[0] = (column(0) + pltpu.roll(column(1), 1, 0)).reshape(NB, 2, 16, L)
    pack(bfield, bsend)
    start_turn(bsend, bext, s_b, r_b)
    end_turn(bsend, bext, s_b, r_b)

    dots[...] = jnp.zeros_like(dots)

    def add_dot(n, a, b):
        dots[n] += jnp.sum((a * b).reshape(16, 8, L), axis=0)

    def b_chunk(f, rows, c):
        v = ysweep([bext[0, j, f, rows, :] for j in range(3)], c, last, first)
        for j in range(3):
            gbuf[j, f, rows, :] = v[j]

    chunks(b_chunk)

    def residual_tile(j, f):
        r = xsweep(gbuf[j, f], cc[j, 2]) - abuf[j, f]
        rbuf[j, f] = r

        @pl.when(j < 2)
        def _():
            add_dot(0, r, r)

        ubuf[j, f] = xsweep(r, cc[j, 2])

    tiles(6, residual_tile)

    def full_chunk(f, rows, c):
        u = ysweep([ubuf[j, f, rows, :] for j in range(3)], c, last, first)
        v = [tri(u[j], text[0, j, f, rows, :], text[1, j, f, rows, :]) for j in range(3)]
        v = ysweep(v, c, last, first)
        for j in range(3):
            gbuf[j, f, rows, :] = v[j]

    chunks(full_chunk)

    def q_tile(j, f):
        r = rbuf[j, f]
        q = r + xsweep(gbuf[j, f], cc[j, 2])
        qbuf[j, f] = q

        @pl.when(j < 2)
        def _():
            add_dot(1, r, q)
            add_dot(2, q, q)

        ubuf[j, f] = xsweep(q, cc[j, 2])

    tiles(6, q_tile)
    chunks(full_chunk)

    def p_tile(j, f):
        q = qbuf[j, f]
        p = q + xsweep(gbuf[j, f], cc[j, 2])
        abuf[j, f] = p
        add_dot(3, q, p)

    tiles(4, p_tile)

    lines = [jnp.sum(dots[n], axis=0, keepdims=True) for n in range(4)]
    red1[0] = jnp.concatenate(lines + [jnp.zeros((4, L), f32)], axis=0)

    def sum1(k):
        return pltpu.make_async_remote_copy(
            src_ref=red1.at[0], dst_ref=red1.at[k], send_sem=s_1.at[k], recv_sem=r_1.at[k],
            device_id={"px": ypeer(k)}, device_id_type=MESH,
        )

    def sum2(k):
        return pltpu.make_async_remote_copy(
            src_ref=red2.at[0], dst_ref=red2.at[k], send_sem=s_2.at[k], recv_sem=r_2.at[k],
            device_id={"py": opeer(k)}, device_id_type=MESH,
        )

    for k in range(1, NPX):
        sum1(k).start()
    for k in range(1, NPX):
        sum1(k).wait_recv()
    total = red1[0]
    for k in range(1, NPX):
        total = total + red1[k]
    red2[0] = total
    for k in range(1, NPY):
        sum2(k).start()
    for k in range(1, NPY):
        sum2(k).wait_recv()
    total = red2[0]
    for k in range(1, NPY):
        total = total + red2[k]
    sums = jnp.sum(total, axis=1, keepdims=True)
    rr, rq, qq, qp = [sums[n:n + 1, :] for n in range(4)]
    alpha = rr / rq
    new = alpha * (alpha * qq) - rr
    beta = new / rr
    grow = 1.0 + beta
    alpha2 = new / (grow * grow * rq - 2.0 * alpha * grow * qq + alpha * alpha * qp)
    kr = alpha + alpha2 * grow
    kq = -alpha2 * alpha

    for j in range(2):
        for f in range(2):
            r = rbuf[j, f]
            q = qbuf[j, f]
            ctl[f, :, j * L:(j + 1) * L] = cc[j, f] + kr * r + kq * q
            res[f, :, j * L:(j + 1) * L] = r - kr * q - kq * abuf[j, f]

    for side in range(2):
        edge(side).wait_send()

    def drain_px(k, carry):
        sum1(k).wait_send()
        return carry

    def drain_py(k, carry):
        route(sm, rm, k, s_m, r_m).wait_send()
        route(sw, rw, k, s_w, r_w).wait_send()
        route(sd, rd, k, s_d, r_d).wait_send()
        sum2(k).wait_send()
        return carry

    lax.fori_loop(1, NPX, drain_px, 0)
    lax.fori_loop(1, NPY, drain_py, 0)


def shards(control_start, coef_x, coef_y, innovation, obs_weight, interp, obs_owner, cell_key, stencil):
    dma = pltpu.SemaphoreType.DMA
    vm = pltpu.VMEM
    field = vm((3, 2, L, L), f32)
    scratch = [
        vm((L, L), f32), vm((ROWS, 4 * L), bf16), vm((8, ROWS), bf16), vm((CAP, ROWS), bf16),
        vm((NPY, CAP, L), f32), vm((NPY, CAP, L), f32), vm((NPY, 8, CAP), f32),
        vm((NPY, CAP, L), f32), vm((NPY, CAP, L), f32), vm((NPY, 8, CAP), f32),
        vm((4 * CAP, 6 * L), bf16), vm((8, 4 * CAP), f32), vm((T, 6 * L), f32),
        vm((2, NB, 2, 16, L), f32), vm((NPX, 2, 3, 2, 16, L), f32),
        vm((1, NB, 2, 16, L), f32), vm((NPX, 1, 3, 2, 16, L), f32),
        vm((1, NB, 1, 16, L), f32), vm((NPX, 1, 3, 1, 16, L), f32),
        vm((3, 3, L, L), f32), vm((2, 3, L, L), f32),
        vm((2, 3, 2, L, L), f32), vm((1, 3, 2, L, L), f32), vm((1, 3, 1, L, L), f32),
        field, field, field, field, field,
        vm((4, 8, L), f32), vm((NPX, 8, L), f32), vm((NPY, 8, L), f32),
        dma((NPY,)), dma((NPY,)), dma((NPY,)), dma((NPY,)), dma((NPY,)), dma((NPY,)),
        dma((NPX,)), dma((NPX,)), dma((NPX,)), dma((NPX,)), dma((NPX,)), dma((NPX,)),
        dma((2,)), dma((2,)), dma((NPX,)), dma((NPX,)), dma((NPY,)), dma((NPY,)),
    ]
    out = jax.ShapeDtypeStruct((2, L, 2 * L), f32)
    control, residual = pl.pallas_call(
        kernel,
        out_shape=(out, out),
        in_specs=[pl.BlockSpec(memory_space=pltpu.VMEM)] * 9,
        out_specs=(pl.BlockSpec(memory_space=pltpu.VMEM),) * 2,
        scratch_shapes=scratch,
        compiler_params=pltpu.CompilerParams(
            collective_id=0, has_side_effects=True, vmem_limit_bytes=48 * 1024 * 1024
        ),
        name="assimilate",
    )(
        obs_owner.reshape(8, L), cell_key.reshape(8, L), stencil.reshape(8, L), interp.reshape(8, L),
        innovation, obs_weight, control_start.reshape(2, L, 2 * L), coef_x.reshape(L, 2 * L),
        coef_y.reshape(16, NB * L),
    )
    shape = control_start.shape
    return control.reshape(shape), residual.reshape(shape)


def solution(mesh):
    return jax.shard_map(
        shards,
        mesh=mesh,
        in_specs=(
            P(None, "py", None, "px"),
            P("py", None, "px"),
            P("py", "px", None),
            P(("px", "py"), None),
            P(("px", "py"), None),
            P(("px", "py")),
            P(("px", "py"), None),
            P(("px", "py")),
            P(("px", "py")),
        ),
        out_specs=(P(None, "py", None, "px"), P(None, "py", None, "px")),
        check_vma=False,
    )
```

time: 471 us -> 111 us (0.24); the launches traced: 463 us -> 110 us
  blocking collectives: 244 us -> 0 us
  Pallas kernels: 0 us -> 102 us
  matrix products: 63.1 us -> 0 us
  waiting for transfers between devices: 44.8 us -> 0 us
  local copies, waits for them, and re-layouts: 47.9 us -> 7.63 us
  starting transfers between devices: 32.7 us -> 0 us
  other arithmetic: 24.4 us -> 0 us
  between operations: 6.03 us -> 0.67 us
    psum x3 -> x0, blocking collectives: 189 us -> none  [dot_total(): return lax.psum(jnp.sum(left_side * right_side), ('px', 'py'))]
    pallas_call x0 -> x1, Pallas kernels: none -> 102 us  [shards(): pl.pallas_call(kernel, out_shape=(out, out), in_specs=[pl.BlockSpec(memor...]
    dot_general x6 -> x0, matrix products: 63.1 us -> none  [the longest x3 35.4 us: misfit(): lax.dot_general(interp_matrix, weighted, (((0,), (0,)), ((), ())), precis...]
    all_to_all x5 -> x0, blocking collectives: 55.2 us -> none  [the longest x3 34.3 us: adjoint(): lax.all_to_all(diffuse(values_in, coef_y, 3), 'px', split_axis=3, concat_...]
    all_to_all x5 -> x0, waiting for transfers between devices: 44.8 us -> none  [the longest x1 19.9 us: shards(): lax.all_to_all(bucket(obs_weight), 'py', split_axis=0, concat_axis=0, til...]
    all_to_all x5 -> x0, starting transfers between devices: 32.7 us -> none  [the longest x1 8.43 us: shards(): lax.all_to_all(bucket(row_index), 'py', split_axis=0, concat_axis=0, tile...]
    scatter x4 -> x0, local copies, waits for them, and re-layouts: 18.2 us -> none  [bucket(): return jnp.zeros(buf_shape, values_in.dtype).at[slot_target].set(values_in)]
    unnamed x20, local copies, waits for them, and re-layouts: 19.2 us -> 7.63 us
  transfers between devices with their start and end apart: 5 -> 0, of which waited for: 3 -> 0; matrix products, arithmetic and copies ran while one was open for 4% -> 0% of each run, Pallas kernels for 0% -> 0%
where the time goes in v1:
time: 111 us; the launch traced here: 110 us
  Pallas kernels  102 us (92%)
  local copies, waits for them, and re-layouts  7.63 us (7%)
    pallas_call x1, Pallas kernels, shards(): pl.pallas_call(kernel, out_shape=(out, out), in_specs=[pl.BlockSpec(memor...  102 us
    unnamed x20, local copies, waits for them, and re-layouts  7.63 us

profile of v1, /device:TPU:1, one launch (start us, length us, event | category | flops | bytes accessed | tf_op | source)
XLA Modules:
  0.0 110.3 jit_solution(2414282103776811905)
XLA Ops:
  0.6 0.0 copy-start.7
  0.6 0.0 copy-start.6
  0.7 0.0 copy-start.5
  0.7 0.7 copy-done.7
  1.3 0.0 copy-done.6
  1.3 0.0 copy-done.5
  1.4 0.0 copy-start
  1.4 1.0 copy-done
  2.4 0.0 copy-start.1
  2.4 1.0 copy-done.1
  3.4 0.0 copy-start.2
  3.4 0.9 copy-done.2
  4.4 0.0 copy-start.3
  4.4 0.9 copy-done.3
  5.3 0.0 copy-start.4
  5.3 0.9 copy-done.4
  6.2 0.0 copy-start.8
  6.2 0.7 copy-done.8
  6.9 102.0 %assimilate.1 = (f32[2,128,256]{2,1,0:T(8,128)S(1)}, f32[2,128,256]{2,1,0:T(8,128)S(1)}) custom-call(s32[8,128]{1,0:T(8,128)S(1)} %bitcast.18, s32[8,128]{1,0:T(8,128)S(1)} %bitcast.19, s32[8,128]{1,0:T(8,128)S(1)} %bitcast.20, f32[8,128]{1,0:T(8,128)S(1)} %bitcast.21, f32[1024,128]{1,0:T(8,128)S(1)} %copy-done, f32[1024,128]{1,0:T(8,128)S(1)} %copy-done.1, ...), custom_call_target="tpu_custom_call" | custom-call | tf_op jit(solution)/shard_map/assimilate/pallas_call | solution.py:494
  108.9 0.7 copy.15
  109.6 0.7 copy.16
Async XLA Ops:
  0.6 0.7 copy-start.7
  0.6 0.7 copy-start.6
  0.7 0.7 copy-start.5
  1.4 1.0 copy-start
  2.4 1.0 copy-start.1
  3.4 0.9 copy-start.2
  4.4 0.9 copy-start.3
  5.3 0.9 copy-start.4
  6.2 0.7 copy-start.8

commit v2 on v1

--- a/solution.py
+++ b/solution.py
@@ -33,20 +33,55 @@
     return hi, (v - hi.astype(f32)).astype(bf16)
 
 
-def xsweep(v, c):
-    for _ in range(M):
-        flux = c * (pltpu.roll(v, L - 1, 0) - v)
-        v = v + flux - pltpu.roll(flux, 1, 0)
-    return v
-
-
-def ysweep(v, c, last, first):
-    for _ in range(M):
-        r = [pltpu.roll(t, L - 1, 1) for t in v]
-        flux = [c[j] * (jnp.where(last, r[(j + 1) % 3], r[j]) - v[j]) for j in range(3)]
-        r = [pltpu.roll(t, 1, 1) for t in flux]
-        v = [v[j] + flux[j] - jnp.where(first, r[(j + 2) % 3], r[j]) for j in range(3)]
-    return v
+def xshift(v, k):
+    return [pltpu.roll(t, (-k) % L, 0) for t in v] if k else v
+
+
+def yshift(v, k):
+    if k == 0:
+        return v
+    lane = iota(v[0].shape, 1)
+    r = [pltpu.roll(t, (-k) % L, 1) for t in v]
+    n = len(v)
+    if k > 0:
+        return [jnp.where(lane < L - k, r[j], r[(j + 1) % n]) for j in range(n)]
+    return [jnp.where(lane >= -k, r[j], r[(j + n - 1) % n]) for j in range(n)]
+
+
+def mul(a, b):
+    return [x * y for x, y in zip(a, b)]
+
+
+def add(*terms):
+    total = terms[0]
+    for t in terms[1:]:
+        total = [x + y for x, y in zip(total, t)]
+    return total
+
+
+def band(c, shift):
+    a = shift(c, -1)
+    d = [1.0 - x - y for x, y in zip(c, a)]
+    p0 = add(mul(d, d), mul(c, c), mul(a, a))
+    p1 = mul(c, add(d, shift(d, 1)))
+    p2 = mul(c, shift(c, 1))
+    n1, n2 = shift(p1, -1), shift(p2, -2)
+    up1 = shift(p1, 1)
+    b0 = add(mul(p0, p0), mul(p1, p1), mul(p2, p2), mul(n1, n1), mul(n2, n2))
+    b1 = add(mul(p1, add(p0, shift(p0, 1))), mul(p2, up1), mul(n1, shift(p2, -1)))
+    b2 = add(mul(p0, p2), mul(p1, up1), mul(p2, shift(p0, 2)))
+    b3 = add(mul(p1, shift(p2, 1)), mul(p2, shift(p1, 2)))
+    b4 = mul(p2, shift(p2, 2))
+    return [shift(b4, -4), shift(b3, -3), shift(b2, -2), shift(b1, -1), b0, b1, b2, b3, b4]
+
+
+def sweep(w, v, shift, keep=3):
+    total = None
+    for m in range(2 * M + 1):
+        moved = shift(v, m - M)[:keep]
+        term = [w(m, j) * t for j, t in enumerate(moved)]
+        total = term if total is None else add(total, term)
+    return total
 
 
 def tri(u, d, e):
@@ -55,7 +90,8 @@
 
 
 def kernel(
-    own, key, sten, itp, inn, wgt, cin, cxin, cyin, ctl, res,
+    h_own, h_key, h_sten, h_itp, h_inn, h_wgt, h_c, h_cx, h_cy, ctl, res,
+    own, key, sten, itp, inn, wgt, cyin, s_in, wx, wy,
     keys, vals, metaq, pbuf, sw, sd, sm, rw, rd, rm, rhs, tid, acc,
     tfield, tsend, bfield, bsend, cyfield, cysend, cc, halo, text, bext, cyx,
     ubuf, gbuf, abuf, rbuf, qbuf, dots, red1, red2,
@@ -68,9 +104,18 @@
         return lax.rem(px + k, NPX)
 
     def opeer(k):
-        x = lax.rem(py // 4 + k // 4, 4)
-        z = lax.rem(lax.rem(py, 4) + lax.rem(k, 4), 4)
+        x = lax.rem(py // 4 + lax.rem(k, 4), 4)
+        z = lax.rem(lax.rem(py, 4) + k // 4 + 4 - lax.rem(k, 4), 4)
         return x * 4 + z
+
+    loads = [(h_own, own), (h_key, key), (h_sten, sten), (h_itp, itp), (h_wgt, wgt), (h_inn, inn), (h_cy, cyin)]
+    for j in range(2):
+        lanes = slice(j * L, (j + 1) * L)
+        loads.append((h_c.at[:, :, lanes], cc.at[j, 0:2]))
+        loads.append((h_cx.at[:, lanes], cc.at[j, 2]))
+    loads = [pltpu.make_async_copy(a, b, s_in.at[n]) for n, (a, b) in enumerate(loads)]
+    for load in loads:
+        load.start()
 
     barrier = pltpu.get_barrier_semaphore()
 
@@ -85,6 +130,8 @@
     lax.fori_loop(1, NPX, greet_px, 0)
     lax.fori_loop(1, NPY, greet_py, 0)
 
+    for n in range(4):
+        loads[n].wait()
     row = iota((L, L), 0)
     col = iota((L, L), 1)
     owner = own[...]
@@ -110,6 +157,9 @@
         pick = [t[bl:bl + 1, :] for t in (s_hi, s_mid, s_lo, fx, seg)] + [zero]
         metaq[:, bl * L:(bl + 1) * L] = jnp.concatenate(pick, axis=0).astype(bf16)
 
+    loads[4].wait()
+    loads[5].wait()
+
     def cut(i, carry):
         rows = pl.ds(pl.multiple_of(i * L, L), L)
         w = wgt[rows, :]
@@ -123,11 +173,11 @@
 
     lax.fori_loop(0, 8, cut, 0)
 
-    rowmask = iota((L, L), 0) < L - 1
+    for load in loads[6:]:
+        load.wait()
     for j in range(2):
-        for f in range(2):
-            cc[j, f] = cin[f, :, j * L:(j + 1) * L]
-        cc[j, 2] = jnp.where(rowmask, cxin[:, j * L:(j + 1) * L], 0.0)
+        tail = cc[j, 2, L - 8:L, :]
+        cc[j, 2, L - 8:L, :] = jnp.where(iota((8, L), 0) < 7, tail, 0.0)
     lanes16 = iota((16, L), 1)
     for b in range(NB):
         tile = cyin[:, b * L:(b + 1) * L]
@@ -225,11 +275,6 @@
 
     lax.fori_loop(1, NPY, send_rows, 0)
 
-    def send_data(k, carry):
-        route(sd, rd, k, s_d, r_d).start()
-        return carry
-
-    lax.fori_loop(1, NPY, send_data, 0)
     meta, w, wd = gather(0)
     rm[0] = meta
     rw[0] = w
@@ -242,36 +287,63 @@
         cc[2, f] = jnp.where(lanes < 64, halo[0, f], halo[1, f])
     end_turn(cysend, cyx, s_c, r_c)
 
-    last = iota((16, L), 1) == L - 1
-    first = iota((16, L), 1) == 0
+    CH = 32
 
     def tiles(count, body):
-        def one(t, carry):
-            body(t // 2, lax.rem(t, 2))
+        def one(j, carry):
+            for f in range(2):
+                body(j, f)
             return carry
 
         lax.fori_loop(0, count, one, 0)
 
     def chunks(body):
         def one(i, carry):
-            rows = pl.ds(pl.multiple_of(i * 16, 16), 16)
-            c = [cyx[0, j, 0, rows, :] for j in range(3)]
+            rows = pl.ds(pl.multiple_of(i * CH, CH), CH)
             for f in range(2):
-                body(f, rows, c)
+                body(f, rows)
             return carry
 
-        lax.fori_loop(0, 8, one, 0)
+        lax.fori_loop(0, L // CH, one, 0)
+
+    def bands_x(j, carry):
+        for m, w in enumerate(band([cc[j, 2]], xshift)):
+            wx[m, j] = w[0]
+        return carry
+
+    def bands_y(i, carry):
+        rows = pl.ds(pl.multiple_of(i * 16, 16), 16)
+        for m, w in enumerate(band([cyx[0, j, 0, rows, :] for j in range(3)], yshift)):
+            for j in range(3):
+                wy[m, j, rows, :] = w[j]
+        return carry
+
+    lax.fori_loop(0, 3, bands_x, 0)
+    lax.fori_loop(0, 8, bands_y, 0)
+
+    def sweep_x(v, j):
+        return sweep(lambda m, _: wx[m, j], [v], xshift)[0]
+
+    def sweep_y(v, rows, keep=3):
+        return sweep(lambda m, j: wy[m, j, rows, :], v, yshift, keep)
 
     def first_x(j, f):
-        ubuf[j, f] = xsweep(cc[j, f], cc[j, 2])
-
-    def first_y(f, rows, c):
-        v = ysweep([ubuf[j, f, rows, :] for j in range(3)], c, last, first)
+        ubuf[j, f] = sweep_x(cc[j, f], j)
+
+    def first_y(f, rows):
+        v = sweep_y([ubuf[j, f, rows, :] for j in range(3)], rows)
         for j in range(3):
             ubuf[j, f, rows, :] = v[j]
 
-    tiles(6, first_x)
+    tiles(3, first_x)
     chunks(first_y)
+
+    def send_data(k, carry):
+        route(sw, rw, k, s_w, r_w).wait_send()
+        route(sd, rd, k, s_d, r_d).start()
+        return carry
+
+    lax.fori_loop(1, NPY, send_data, 0)
 
     pick = jnp.where(iota((8, L), 0) < 3, 1.0, 0.0).astype(bf16)
     target = iota((T, 4 * CAP), 0).astype(f32)
@@ -323,27 +395,30 @@
     tfield[1] = column(2).reshape(NB, 2, 16, L)
     pack(tfield, tsend)
     start_turn(tsend, text, s_t, r_t)
+
+    def d_group(g, carry):
+        group(g, rd, sd, s_d, r_d, False, 2)
+        return carry
+
+    lax.fori_loop(0, 1, d_group, 0)
     end_turn(tsend, text, s_t, r_t)
 
-    def mid_chunk(f, rows, c):
+    def spread(f, rows, keep=3):
         u = [ubuf[j, f, rows, :] for j in range(3)]
-        v = [tri(u[j], text[0, j, f, rows, :], text[1, j, f, rows, :]) for j in range(3)]
-        v = ysweep(v, c, last, first)
+        return u, [tri(u[j], text[0, j, f, rows, :], text[1, j, f, rows, :]) for j in range(3)]
+
+    def mid_chunk(f, rows):
+        v = sweep_y(spread(f, rows)[1], rows)
         for j in range(3):
             gbuf[j, f, rows, :] = v[j]
 
     chunks(mid_chunk)
 
     def image_start(j, f):
-        abuf[j, f] = cc[j, f] + xsweep(gbuf[j, f], cc[j, 2])
-
-    tiles(6, image_start)
-
-    def d_group(g, carry):
-        group(g, rd, sd, s_d, r_d, False, 2)
-        return carry
-
-    lax.fori_loop(0, 4, d_group, 0)
+        abuf[j, f] = cc[j, f] + sweep_x(gbuf[j, f], j)
+
+    tiles(3, image_start)
+    lax.fori_loop(1, 4, d_group, 0)
     bfield[0] = (column(0) + pltpu.roll(column(1), 1, 0)).reshape(NB, 2, 16, L)
     pack(bfield, bsend)
     start_turn(bsend, bext, s_b, r_b)
@@ -352,58 +427,67 @@
     dots[...] = jnp.zeros_like(dots)
 
     def add_dot(n, a, b):
-        dots[n] += jnp.sum((a * b).reshape(16, 8, L), axis=0)
-
-    def b_chunk(f, rows, c):
-        v = ysweep([bext[0, j, f, rows, :] for j in range(3)], c, last, first)
+        dots[n] += jnp.sum((a * b).reshape(-1, 8, L), axis=0)
+
+    def b_chunk(f, rows):
+        v = sweep_y([bext[0, j, f, rows, :] for j in range(3)], rows)
         for j in range(3):
             gbuf[j, f, rows, :] = v[j]
 
     chunks(b_chunk)
 
     def residual_tile(j, f):
-        r = xsweep(gbuf[j, f], cc[j, 2]) - abuf[j, f]
+        r = sweep_x(gbuf[j, f], j) - abuf[j, f]
         rbuf[j, f] = r
 
         @pl.when(j < 2)
         def _():
             add_dot(0, r, r)
 
-        ubuf[j, f] = xsweep(r, cc[j, 2])
-
-    tiles(6, residual_tile)
-
-    def full_chunk(f, rows, c):
-        u = ysweep([ubuf[j, f, rows, :] for j in range(3)], c, last, first)
+        ubuf[j, f] = sweep_x(r, j)
+
+    tiles(3, residual_tile)
+
+    def q_chunk(f, rows):
+        u = sweep_y([ubuf[j, f, rows, :] for j in range(3)], rows)
         v = [tri(u[j], text[0, j, f, rows, :], text[1, j, f, rows, :]) for j in range(3)]
-        v = ysweep(v, c, last, first)
+        for j in range(2):
+            add_dot(1, u[j], v[j])
+        v = sweep_y(v, rows)
         for j in range(3):
             gbuf[j, f, rows, :] = v[j]
 
-    chunks(full_chunk)
+    chunks(q_chunk)
 
     def q_tile(j, f):
-        r = rbuf[j, f]
-        q = r + xsweep(gbuf[j, f], cc[j, 2])
+        q = rbuf[j, f] + sweep_x(gbuf[j, f], j)
         qbuf[j, f] = q
 
         @pl.when(j < 2)
         def _():
-            add_dot(1, r, q)
             add_dot(2, q, q)
 
-        ubuf[j, f] = xsweep(q, cc[j, 2])
-
-    tiles(6, q_tile)
-    chunks(full_chunk)
+        ubuf[j, f] = sweep_x(q, j)
+
+    tiles(3, q_tile)
+
+    def p_up(f, rows):
+        u = sweep_y([ubuf[j, f, rows, :] for j in range(3)], rows)
+        v = [tri(u[j], text[0, j, f, rows, :], text[1, j, f, rows, :]) for j in range(3)]
+        for j in range(2):
+            add_dot(3, u[j], v[j])
+        for j in range(3):
+            ubuf[j, f, rows, :] = v[j]
+
+    chunks(p_up)
+
+    def p_down(f, rows):
+        v = sweep_y([ubuf[j, f, rows, :] for j in range(3)], rows, 2)
+        for j in range(2):
+            gbuf[j, f, rows, :] = v[j]
 
     def p_tile(j, f):
-        q = qbuf[j, f]
-        p = q + xsweep(gbuf[j, f], cc[j, 2])
-        abuf[j, f] = p
-        add_dot(3, q, p)
-
-    tiles(4, p_tile)
+        abuf[j, f] = qbuf[j, f] + sweep_x(gbuf[j, f], j)
 
     lines = [jnp.sum(dots[n], axis=0, keepdims=True) for n in range(4)]
     red1[0] = jnp.concatenate(lines + [jnp.zeros((4, L), f32)], axis=0)
@@ -422,6 +506,7 @@
 
     for k in range(1, NPX):
         sum1(k).start()
+    chunks(p_down)
     for k in range(1, NPX):
         sum1(k).wait_recv()
     total = red1[0]
@@ -430,13 +515,16 @@
     red2[0] = total
     for k in range(1, NPY):
         sum2(k).start()
+    tiles(2, p_tile)
     for k in range(1, NPY):
         sum2(k).wait_recv()
     total = red2[0]
     for k in range(1, NPY):
         total = total + red2[k]
     sums = jnp.sum(total, axis=1, keepdims=True)
-    rr, rq, qq, qp = [sums[n:n + 1, :] for n in range(4)]
+    rr, gain, qq, gain2 = [sums[n:n + 1, :] for n in range(4)]
+    rq = rr + gain
+    qp = qq + gain2
     alpha = rr / rq
     new = alpha * (alpha * qq) - rr
     beta = new / rr
@@ -461,7 +549,6 @@
 
     def drain_py(k, carry):
         route(sm, rm, k, s_m, r_m).wait_send()
-        route(sw, rw, k, s_w, r_w).wait_send()
         route(sd, rd, k, s_d, r_d).wait_send()
         sum2(k).wait_send()
         return carry
@@ -475,6 +562,9 @@
     vm = pltpu.VMEM
     field = vm((3, 2, L, L), f32)
     scratch = [
+        vm((8, L), jnp.int32), vm((8, L), jnp.int32), vm((8, L), jnp.int32), vm((8, L), f32),
+        vm((ROWS, L), f32), vm((ROWS, L), f32), vm((16, NB * L), f32), dma((11,)),
+        vm((2 * M + 1, 3, L, L), f32), vm((2 * M + 1, 3, L, L), f32),
         vm((L, L), f32), vm((ROWS, 4 * L), bf16), vm((8, ROWS), bf16), vm((CAP, ROWS), bf16),
         vm((NPY, CAP, L), f32), vm((NPY, CAP, L), f32), vm((NPY, 8, CAP), f32),
         vm((NPY, CAP, L), f32), vm((NPY, CAP, L), f32), vm((NPY, 8, CAP), f32),
@@ -494,11 +584,11 @@
     control, residual = pl.pallas_call(
         kernel,
         out_shape=(out, out),
-        in_specs=[pl.BlockSpec(memory_space=pltpu.VMEM)] * 9,
+        in_specs=[pl.BlockSpec(memory_space=pltpu.HBM)] * 9,
         out_specs=(pl.BlockSpec(memory_space=pltpu.VMEM),) * 2,
         scratch_shapes=scratch,
         compiler_params=pltpu.CompilerParams(
-            collective_id=0, has_side_effects=True, vmem_limit_bytes=48 * 1024 * 1024
+            collective_id=0, has_side_effects=True, vmem_limit_bytes=60 * 1024 * 1024
         ),
         name="assimilate",
     )(

time: 111 us -> 85.8 us (0.77)
  Pallas kernels: 102 us -> 82.5 us
  local copies, waits for them, and re-layouts: 7.63 us -> 2.42 us
    pallas_call x1, Pallas kernels: 102 us -> 82.5 us  [shards(): pl.pallas_call(kernel, out_shape=(out, out), in_specs=[pl.BlockSpec(memor...]
    unnamed x20 -> x4, local copies, waits for them, and re-layouts: 7.63 us -> 2.42 us
where the time goes in v2:
time: 85.8 us; the launch traced here: 85.6 us
  Pallas kernels  82.5 us (96%)
  local copies, waits for them, and re-layouts  2.42 us (3%)
    pallas_call x1, Pallas kernels, shards(): pl.pallas_call(kernel, out_shape=(out, out), in_specs=[pl.BlockSpec(memor...  82.5 us
    unnamed x4, local copies, waits for them, and re-layouts  2.42 us

profile of v2, /device:TPU:1, one launch (start us, length us, event | category | flops | bytes accessed | tf_op | source)
XLA Modules:
  0.0 85.6 jit_solution(16996921329866444960)
XLA Ops:
  0.6 82.5 %assimilate.1 = (f32[2,128,256]{2,1,0:T(8,128)}, f32[2,128,256]{2,1,0:T(8,128)}) custom-call(s32[8,128]{1,0:T(8,128)} %bitcast.18, s32[8,128]{1,0:T(8,128)} %bitcast.19, s32[8,128]{1,0:T(8,128)} %bitcast.20, f32[8,128]{1,0:T(8,128)} %bitcast.21, f32[1024,128]{1,0:T(8,128)} %h_inn.1, f32[1024,128]{1,0:T(8,128)} %h_wgt.1, f32[2,128,256]{2,1,0:T(8,128)} %bitcast.13, ...), custom_call_target="tpu_custom_call" | custom-call | tf_op jit(solution)/shard_map/assimilate/pallas_call | solution.py:584
  83.2 0.0 copy-start
  83.2 1.7 %copy.15 = f32[2,1,128,256]{3,2,1,0:T(8,128)} copy(f32[2,1,128,256]{3,2,1,0:T(8,128)} %bitcast.15) | data formatting | bytes 524288
  84.9 0.0 copy-done
  84.9 0.7 copy.16
Async XLA Ops:
  83.2 1.7 %copy-start = (f32[2,128,256]{2,1,0:T(8,128)S(1)}, f32[2,128,256]{2,1,0:T(8,128)}, u32[]{:S(2)}) copy-start(f32[2,128,256]{2,1,0:T(8,128)} %get-tuple-element.5) | copy-start | bytes 786436

commit v3 on v2

--- a/solution.py
+++ b/solution.py
@@ -104,6 +104,7 @@
         return lax.rem(px + k, NPX)
 
     def opeer(k):
+        k = lax.rem(k + lax.rem(px, 2) * (2 * NPY - 2 * k), NPY)
         x = lax.rem(py // 4 + lax.rem(k, 4), 4)
         z = lax.rem(lax.rem(py, 4) + k // 4 + 4 - lax.rem(k, 4), 4)
         return x * 4 + z
@@ -400,7 +401,10 @@
         group(g, rd, sd, s_d, r_d, False, 2)
         return carry
 
-    lax.fori_loop(0, 1, d_group, 0)
+    lax.fori_loop(0, 4, d_group, 0)
+    bfield[0] = (column(0) + pltpu.roll(column(1), 1, 0)).reshape(NB, 2, 16, L)
+    pack(bfield, bsend)
+    start_turn(bsend, bext, s_b, r_b)
     end_turn(tsend, text, s_t, r_t)
 
     def spread(f, rows, keep=3):
@@ -418,10 +422,6 @@
         abuf[j, f] = cc[j, f] + sweep_x(gbuf[j, f], j)
 
     tiles(3, image_start)
-    lax.fori_loop(1, 4, d_group, 0)
-    bfield[0] = (column(0) + pltpu.roll(column(1), 1, 0)).reshape(NB, 2, 16, L)
-    pack(bfield, bsend)
-    start_turn(bsend, bext, s_b, r_b)
     end_turn(bsend, bext, s_b, r_b)
 
     dots[...] = jnp.zeros_like(dots)

time: 85.8 us -> 77.3 us (0.901)
  Pallas kernels: 82.5 us -> 74.1 us
    pallas_call x1, Pallas kernels: 82.5 us -> 74.1 us  [shards(): pl.pallas_call(kernel, out_shape=(out, out), in_specs=[pl.BlockSpec(memor...]
where the time goes in v3:
time: 77.3 us; the launch traced here: 77.1 us
  Pallas kernels  74.1 us (96%)
  local copies, waits for them, and re-layouts  2.42 us (3%)
    pallas_call x1, Pallas kernels, shards(): pl.pallas_call(kernel, out_shape=(out, out), in_specs=[pl.BlockSpec(memor...  74.1 us
    unnamed x4, local copies, waits for them, and re-layouts  2.42 us

profile of v3, /device:TPU:1, one launch (start us, length us, event | category | flops | bytes accessed | tf_op | source)
XLA Modules:
  0.0 77.1 jit_solution(59088248647353149)
XLA Ops:
  0.6 74.1 %assimilate.1 = (f32[2,128,256]{2,1,0:T(8,128)}, f32[2,128,256]{2,1,0:T(8,128)}) custom-call(s32[8,128]{1,0:T(8,128)} %bitcast.18, s32[8,128]{1,0:T(8,128)} %bitcast.19, s32[8,128]{1,0:T(8,128)} %bitcast.20, f32[8,128]{1,0:T(8,128)} %bitcast.21, f32[1024,128]{1,0:T(8,128)} %h_inn.1, f32[1024,128]{1,0:T(8,128)} %h_wgt.1, f32[2,128,256]{2,1,0:T(8,128)} %bitcast.13, ...), custom_call_target="tpu_custom_call" | custom-call | tf_op jit(solution)/shard_map/assimilate/pallas_call | solution.py:584
  74.7 0.0 copy-start
  74.7 1.7 %copy.15 = f32[2,1,128,256]{3,2,1,0:T(8,128)} copy(f32[2,1,128,256]{3,2,1,0:T(8,128)} %bitcast.15) | data formatting | bytes 524288
  76.4 0.0 copy-done
  76.4 0.7 copy.16
Async XLA Ops:
  74.7 1.7 %copy-start = (f32[2,128,256]{2,1,0:T(8,128)S(1)}, f32[2,128,256]{2,1,0:T(8,128)}, u32[]{:S(2)}) copy-start(f32[2,128,256]{2,1,0:T(8,128)} %get-tuple-element.5) | copy-start | bytes 786436

commit v4 on v3

--- a/solution.py
+++ b/solution.py
@@ -94,7 +94,7 @@
     own, key, sten, itp, inn, wgt, cyin, s_in, wx, wy,
     keys, vals, metaq, pbuf, sw, sd, sm, rw, rd, rm, rhs, tid, acc,
     tfield, tsend, bfield, bsend, cyfield, cysend, cc, halo, text, bext, cyx,
-    ubuf, gbuf, abuf, rbuf, qbuf, dots, red1, red2,
+    ubuf, gbuf, abuf, rbuf, qbuf, dots, red1, red2, onehot, shares_of,
     s_m, s_w, s_d, r_m, r_w, r_d, s_t, r_t, s_b, r_b, s_c, r_c, s_h, r_h, s_1, r_1, s_2, r_2,
 ):
     px = lax.axis_index("px")
@@ -128,8 +128,10 @@
         pl.semaphore_signal(barrier, inc=1, device_id={"py": opeer(k)}, device_id_type=MESH)
         return carry
 
-    lax.fori_loop(1, NPX, greet_px, 0)
-    lax.fori_loop(1, NPY, greet_py, 0)
+    for k in range(1, NPX):
+        greet_px(k, 0)
+    for k in range(1, NPY):
+        greet_py(k, 0)
 
     for n in range(4):
         loads[n].wait()
@@ -174,6 +176,94 @@
 
     lax.fori_loop(0, 8, cut, 0)
 
+    def pack(field, out):
+        def one(p, carry):
+            out[p, :, 0] = field[:, 2 * p]
+            out[p, :, 1] = field[:, 2 * p + 1]
+            right = field[:, lax.rem(2 * p + 2, NB)]
+            left = field[:, lax.rem(2 * p + NB - 1, NB)]
+            out[p, :, 2] = jnp.where(iota(right.shape, right.ndim - 1) < 64, right, left)
+            return carry
+
+        lax.fori_loop(0, NPX, one, 0)
+
+    def block(ext, k):
+        return ext.at[:, :, :, pl.ds(pl.multiple_of(k * 16, 16), 16), :]
+
+    def turn(send, ext, k, ssem, rsem):
+        return pltpu.make_async_remote_copy(
+            src_ref=send.at[ypeer(k)], dst_ref=block(ext, px),
+            send_sem=ssem.at[k], recv_sem=rsem.at[k],
+            device_id={"px": ypeer(k)}, device_id_type=MESH,
+        )
+
+    def turned(send, ext, k, ssem, rsem):
+        source = lax.rem(px + NPX - k, NPX)
+        return pltpu.make_async_remote_copy(
+            src_ref=send.at[source], dst_ref=block(ext, source),
+            send_sem=ssem.at[k], recv_sem=rsem.at[k],
+            device_id={"px": ypeer(k)}, device_id_type=MESH,
+        )
+
+    def start_turn(send, ext, ssem, rsem):
+        def one(k, carry):
+            turn(send, ext, k, ssem, rsem).start()
+            return carry
+
+        lax.fori_loop(1, NPX, one, 0)
+        ext[:, :, :, pl.ds(pl.multiple_of(px * 16, 16), 16), :] = send[px]
+
+    def end_turn(send, ext, ssem, rsem):
+        def one(k, carry):
+            turned(send, ext, k, ssem, rsem).wait_recv()
+            return carry
+
+        lax.fori_loop(1, NPX, one, 0)
+
+    pl.semaphore_wait(barrier, NPX - 1 + NPY - 1)
+
+    def edge(side):
+        peer = ypeer(1 if side == 1 else NPX - 1)
+        return pltpu.make_async_remote_copy(
+            src_ref=cc.at[side], dst_ref=halo.at[side],
+            send_sem=s_h.at[side], recv_sem=r_h.at[side],
+            device_id={"px": peer}, device_id_type=MESH,
+        )
+
+    def route(buf, land, k, ssem, rsem):
+        return pltpu.make_async_remote_copy(
+            src_ref=buf.at[k], dst_ref=land.at[k],
+            send_sem=ssem.at[k], recv_sem=rsem.at[k],
+            device_id={"py": opeer(k)}, device_id_type=MESH,
+        )
+
+    slot = iota((CAP, L), 0).astype(f32)
+
+    def gather(k):
+        base = pl.multiple_of(opeer(k) * 8, 8)
+        mine = keys[pl.ds(base, 8), :]
+        for bl in range(8):
+            pbuf[:, bl * L:(bl + 1) * L] = (slot == mine[bl:bl + 1, :]).astype(f32).astype(bf16)
+        meta = lax.dot_general(metaq[...], pbuf[...], NT, preferred_element_type=f32)
+        out = dot(pbuf[...], vals[...])
+        return meta, out[:, 0:L] + out[:, L:2 * L], out[:, 2 * L:3 * L] + out[:, 3 * L:4 * L]
+
+    def send_rows(k, carry):
+        meta, w, wd = gather(k)
+        sm[k] = meta
+        sw[k] = w
+        sd[k] = wd
+        route(sm, rm, k, s_m, r_m).start()
+        route(sw, rw, k, s_w, r_w).start()
+        return carry
+
+    lax.fori_loop(1, NPY, send_rows, 0)
+
+    meta, w, wd = gather(0)
+    rm[0] = meta
+    rw[0] = w
+    rd[0] = wd
+
     for load in loads[6:]:
         load.wait()
     for j in range(2):
@@ -186,100 +276,18 @@
             tile = jnp.where(lanes16 < L - 1, tile, 0.0)
         cyfield[0, b, 0] = tile
 
-    def pack(field, out):
-        def one(p, carry):
-            out[p, :, 0] = field[:, 2 * p]
-            out[p, :, 1] = field[:, 2 * p + 1]
-            right = field[:, lax.rem(2 * p + 2, NB)]
-            left = field[:, lax.rem(2 * p + NB - 1, NB)]
-            out[p, :, 2] = jnp.where(iota(right.shape, right.ndim - 1) < 64, right, left)
-            return carry
-
-        lax.fori_loop(0, NPX, one, 0)
-
-    def block(ext, k):
-        return ext.at[:, :, :, pl.ds(pl.multiple_of(k * 16, 16), 16), :]
-
-    def turn(send, ext, k, ssem, rsem):
-        return pltpu.make_async_remote_copy(
-            src_ref=send.at[ypeer(k)], dst_ref=block(ext, px),
-            send_sem=ssem.at[k], recv_sem=rsem.at[k],
-            device_id={"px": ypeer(k)}, device_id_type=MESH,
-        )
-
-    def turned(send, ext, k, ssem, rsem):
-        source = lax.rem(px + NPX - k, NPX)
-        return pltpu.make_async_remote_copy(
-            src_ref=send.at[source], dst_ref=block(ext, source),
-            send_sem=ssem.at[k], recv_sem=rsem.at[k],
-            device_id={"px": ypeer(k)}, device_id_type=MESH,
-        )
-
-    def start_turn(send, ext, ssem, rsem):
+    def free_turn(send, ext, ssem, rsem):
         def one(k, carry):
-            turn(send, ext, k, ssem, rsem).start()
-            return carry
-
-        lax.fori_loop(1, NPX, one, 0)
-        ext[:, :, :, pl.ds(pl.multiple_of(px * 16, 16), 16), :] = send[px]
-
-    def end_turn(send, ext, ssem, rsem):
-        def one(k, carry):
-            turned(send, ext, k, ssem, rsem).wait_recv()
             turn(send, ext, k, ssem, rsem).wait_send()
             return carry
 
         lax.fori_loop(1, NPX, one, 0)
 
     pack(cyfield, cysend)
-
-    pl.semaphore_wait(barrier, NPX - 1 + NPY - 1)
-
-    def edge(side):
-        peer = ypeer(1 if side == 1 else NPX - 1)
-        return pltpu.make_async_remote_copy(
-            src_ref=cc.at[side], dst_ref=halo.at[side],
-            send_sem=s_h.at[side], recv_sem=r_h.at[side],
-            device_id={"px": peer}, device_id_type=MESH,
-        )
 
     edge(0).start()
     edge(1).start()
     start_turn(cysend, cyx, s_c, r_c)
-
-    def route(buf, land, k, ssem, rsem):
-        return pltpu.make_async_remote_copy(
-            src_ref=buf.at[k], dst_ref=land.at[k],
-            send_sem=ssem.at[k], recv_sem=rsem.at[k],
-            device_id={"py": opeer(k)}, device_id_type=MESH,
-        )
-
-    slot = iota((CAP, L), 0).astype(f32)
-
-    def gather(k):
-        base = pl.multiple_of(opeer(k) * 8, 8)
-        mine = keys[pl.ds(base, 8), :]
-        for bl in range(8):
-            pbuf[:, bl * L:(bl + 1) * L] = (slot == mine[bl:bl + 1, :]).astype(f32).astype(bf16)
-        meta = lax.dot_general(metaq[...], pbuf[...], NT, preferred_element_type=f32)
-        out = dot(pbuf[...], vals[...])
-        return meta, out[:, 0:L] + out[:, L:2 * L], out[:, 2 * L:3 * L] + out[:, 3 * L:4 * L]
-
-    def send_rows(k, carry):
-        meta, w, wd = gather(k)
-        sm[k] = meta
-        sw[k] = w
-        sd[k] = wd
-        route(sm, rm, k, s_m, r_m).start()
-        route(sw, rw, k, s_w, r_w).start()
-        return carry
-
-    lax.fori_loop(1, NPY, send_rows, 0)
-
-    meta, w, wd = gather(0)
-    rm[0] = meta
-    rw[0] = w
-    rd[0] = wd
 
     for side in range(2):
         edge(side).wait_recv()
@@ -288,7 +296,7 @@
         cc[2, f] = jnp.where(lanes < 64, halo[0, f], halo[1, f])
     end_turn(cysend, cyx, s_c, r_c)
 
-    CH = 32
+    CH = 64
 
     def tiles(count, body):
         def one(j, carry):
@@ -340,6 +348,7 @@
     chunks(first_y)
 
     def send_data(k, carry):
+        route(sm, rm, k, s_m, r_m).wait_send()
         route(sw, rw, k, s_w, r_w).wait_send()
         route(sd, rd, k, s_d, r_d).start()
         return carry
@@ -359,21 +368,26 @@
                     route(sm, rm, k, s_m, r_m).wait_recv()
                 route(buf, land, k, ssem, rsem).wait_recv()
 
-            meta = rm[k]
-            s = lax.dot_general(meta.astype(bf16), pick, TN, preferred_element_type=f32)
+            rows = slice(i * CAP, (i + 1) * CAP)
+            if with_meta:
+                meta = rm[k]
+                s = lax.dot_general(meta.astype(bf16), pick, TN, preferred_element_type=f32)
+                shares_of[k] = s
+                tid[0:1, rows] = meta[4:5, :] * 32.0 + meta[3:4, :]
+            else:
+                s = shares_of[k]
             v = land[k]
             va = v * (1.0 - s)
             vs = v * s
             terms = (va * (1.0 - s), vs * s, vs * (1.0 - s)) if parts == 3 else (va, vs)
-            rows = slice(i * CAP, (i + 1) * CAP)
             for n, term in enumerate(terms):
                 hi, lo = split(term)
                 rhs[rows, 2 * n * L:(2 * n + 1) * L] = hi
                 rhs[rows, (2 * n + 1) * L:(2 * n + 2) * L] = lo
-            tid[0:1, rows] = meta[4:5, :] * 32.0 + meta[3:4, :]
-        onehot = (target == tid[0:1, :]).astype(f32).astype(bf16)
+        if with_meta:
+            onehot[g] = (target == tid[0:1, :]).astype(f32).astype(bf16)
         width = 2 * parts * L
-        part = dot(onehot, rhs[:, 0:width])
+        part = dot(onehot[g], rhs[:, 0:width])
 
         @pl.when(g == 0)
         def _():
@@ -405,6 +419,14 @@
     bfield[0] = (column(0) + pltpu.roll(column(1), 1, 0)).reshape(NB, 2, 16, L)
     pack(bfield, bsend)
     start_turn(bsend, bext, s_b, r_b)
+
+    def drain_py(k, carry):
+        route(sd, rd, k, s_d, r_d).wait_send()
+        return carry
+
+    for side in range(2):
+        edge(side).wait_send()
+    free_turn(cysend, cyx, s_c, r_c)
     end_turn(tsend, text, s_t, r_t)
 
     def spread(f, rows, keep=3):
@@ -422,6 +444,8 @@
         abuf[j, f] = cc[j, f] + sweep_x(gbuf[j, f], j)
 
     tiles(3, image_start)
+    lax.fori_loop(1, NPY, drain_py, 0)
+    free_turn(tsend, text, s_t, r_t)
     end_turn(bsend, bext, s_b, r_b)
 
     dots[...] = jnp.zeros_like(dots)
@@ -504,23 +528,25 @@
             device_id={"py": opeer(k)}, device_id_type=MESH,
         )
 
+    def merge(count, send, buf):
+        for k in range(1, count):
+            send(k).wait_recv()
+        total = buf[0]
+        for k in range(1, count):
+            total = total + buf[k]
+        return total
+
     for k in range(1, NPX):
         sum1(k).start()
     chunks(p_down)
-    for k in range(1, NPX):
-        sum1(k).wait_recv()
-    total = red1[0]
-    for k in range(1, NPX):
-        total = total + red1[k]
-    red2[0] = total
+    free_turn(bsend, bext, s_b, r_b)
+    red2[0] = merge(NPX, sum1, red1)
     for k in range(1, NPY):
         sum2(k).start()
+    for k in range(1, NPX):
+        sum1(k).wait_send()
     tiles(2, p_tile)
-    for k in range(1, NPY):
-        sum2(k).wait_recv()
-    total = red2[0]
-    for k in range(1, NPY):
-        total = total + red2[k]
+    total = merge(NPY, sum2, red2)
     sums = jnp.sum(total, axis=1, keepdims=True)
     rr, gain, qq, gain2 = [sums[n:n + 1, :] for n in range(4)]
     rq = rr + gain
@@ -540,21 +566,8 @@
             ctl[f, :, j * L:(j + 1) * L] = cc[j, f] + kr * r + kq * q
             res[f, :, j * L:(j + 1) * L] = r - kr * q - kq * abuf[j, f]
 
-    for side in range(2):
-        edge(side).wait_send()
-
-    def drain_px(k, carry):
-        sum1(k).wait_send()
-        return carry
-
-    def drain_py(k, carry):
-        route(sm, rm, k, s_m, r_m).wait_send()
-        route(sd, rd, k, s_d, r_d).wait_send()
+    for k in range(1, NPY):
         sum2(k).wait_send()
-        return carry
-
-    lax.fori_loop(1, NPX, drain_px, 0)
-    lax.fori_loop(1, NPY, drain_py, 0)
 
 
 def shards(control_start, coef_x, coef_y, innovation, obs_weight, interp, obs_owner, cell_key, stencil):
@@ -576,6 +589,7 @@
         vm((2, 3, 2, L, L), f32), vm((1, 3, 2, L, L), f32), vm((1, 3, 1, L, L), f32),
         field, field, field, field, field,
         vm((4, 8, L), f32), vm((NPX, 8, L), f32), vm((NPY, 8, L), f32),
+        vm((4, T, 4 * CAP), bf16), vm((NPY, CAP, L), f32),
         dma((NPY,)), dma((NPY,)), dma((NPY,)), dma((NPY,)), dma((NPY,)), dma((NPY,)),
         dma((NPX,)), dma((NPX,)), dma((NPX,)), dma((NPX,)), dma((NPX,)), dma((NPX,)),
         dma((2,)), dma((2,)), dma((NPX,)), dma((NPX,)), dma((NPY,)), dma((NPY,)),

time: 77.3 us -> 75.8 us (0.981)
  Pallas kernels: 74.1 us -> 72.6 us
    pallas_call x1, Pallas kernels: 74.1 us -> 72.6 us  [shards(): pl.pallas_call(kernel, out_shape=(out, out), in_specs=[pl.BlockSpec(memor...]
where the time goes in v4:
time: 75.8 us; the launch traced here: 75.6 us
  Pallas kernels  72.6 us (96%)
  local copies, waits for them, and re-layouts  2.42 us (3%)
    pallas_call x1, Pallas kernels, shards(): pl.pallas_call(kernel, out_shape=(out, out), in_specs=[pl.BlockSpec(memor...  72.6 us
    unnamed x4, local copies, waits for them, and re-layouts  2.42 us

profile of v4, /device:TPU:1, one launch (start us, length us, event | category | flops | bytes accessed | tf_op | source)
XLA Modules:
  0.0 75.6 jit_solution(7243259515741998309)
XLA Ops:
  0.6 72.6 %assimilate.1 = (f32[2,128,256]{2,1,0:T(8,128)}, f32[2,128,256]{2,1,0:T(8,128)}) custom-call(s32[8,128]{1,0:T(8,128)} %bitcast.18, s32[8,128]{1,0:T(8,128)} %bitcast.19, s32[8,128]{1,0:T(8,128)} %bitcast.20, f32[8,128]{1,0:T(8,128)} %bitcast.21, f32[1024,128]{1,0:T(8,128)} %h_inn.1, f32[1024,128]{1,0:T(8,128)} %h_wgt.1, f32[2,128,256]{2,1,0:T(8,128)} %bitcast.13, ...), custom_call_target="tpu_custom_call" | custom-call | tf_op jit(solution)/shard_map/assimilate/pallas_call | solution.py:598
  73.2 0.0 copy-start
  73.2 1.7 %copy.15 = f32[2,1,128,256]{3,2,1,0:T(8,128)} copy(f32[2,1,128,256]{3,2,1,0:T(8,128)} %bitcast.15) | data formatting | bytes 524288
  74.9 0.0 copy-done
  74.9 0.7 copy.16
Async XLA Ops:
  73.2 1.7 %copy-start = (f32[2,128,256]{2,1,0:T(8,128)S(1)}, f32[2,128,256]{2,1,0:T(8,128)}, u32[]{:S(2)}) copy-start(f32[2,128,256]{2,1,0:T(8,128)} %get-tuple-element.5) | copy-start | bytes 786436

commit v5 on v4

--- a/solution.py
+++ b/solution.py
@@ -90,12 +90,12 @@
 
 
 def kernel(
-    h_own, h_key, h_sten, h_itp, h_inn, h_wgt, h_c, h_cx, h_cy, ctl, res,
+    h_own, h_key, h_sten, h_itp, h_inn, h_wgt, h_c, h_cx, h_cy, o_r, o_q, o_p, o_k,
     own, key, sten, itp, inn, wgt, cyin, s_in, wx, wy,
     keys, vals, metaq, pbuf, sw, sd, sm, rw, rd, rm, rhs, tid, acc,
     tfield, tsend, bfield, bsend, cyfield, cysend, cc, halo, text, bext, cyx,
     ubuf, gbuf, abuf, rbuf, qbuf, dots, red1, red2, onehot, shares_of,
-    s_m, s_w, s_d, r_m, r_w, r_d, s_t, r_t, s_b, r_b, s_c, r_c, s_h, r_h, s_1, r_1, s_2, r_2,
+    s_m, s_w, s_d, r_m, r_w, r_d, s_t, r_t, s_b, r_b, s_c, r_c, s_h, r_h, s_1, r_1, s_2, r_2, s_o,
 ):
     px = lax.axis_index("px")
     py = lax.axis_index("py")
@@ -244,7 +244,8 @@
         mine = keys[pl.ds(base, 8), :]
         for bl in range(8):
             pbuf[:, bl * L:(bl + 1) * L] = (slot == mine[bl:bl + 1, :]).astype(f32).astype(bf16)
-        meta = lax.dot_general(metaq[...], pbuf[...], NT, preferred_element_type=f32)
+        m = lax.dot_general(metaq[...], pbuf[...], NT, preferred_element_type=f32)
+        meta = jnp.concatenate([m[0:1] + m[1:2] + m[2:3], m[4:5] * 32.0 + m[3:4]], axis=0)
         out = dot(pbuf[...], vals[...])
         return meta, out[:, 0:L] + out[:, L:2 * L], out[:, 2 * L:3 * L] + out[:, 3 * L:4 * L]
 
@@ -258,6 +259,12 @@
         return carry
 
     lax.fori_loop(1, NPY, send_rows, 0)
+
+    def send_data(k, carry):
+        route(sd, rd, k, s_d, r_d).start()
+        return carry
+
+    lax.fori_loop(1, NPY, send_data, 0)
 
     meta, w, wd = gather(0)
     rm[0] = meta
@@ -296,20 +303,21 @@
         cc[2, f] = jnp.where(lanes < 64, halo[0, f], halo[1, f])
     end_turn(cysend, cyx, s_c, r_c)
 
-    CH = 64
-
-    def tiles(count, body):
+    CH = 128
+
+    def tiles(count, body, fields=(0, 1)):
         def one(j, carry):
-            for f in range(2):
+            for f in fields:
                 body(j, f)
             return carry
 
-        lax.fori_loop(0, count, one, 0)
-
-    def chunks(body):
+        for j in range(count):
+            one(j, 0)
+
+    def chunks(body, fields=(0, 1)):
         def one(i, carry):
             rows = pl.ds(pl.multiple_of(i * CH, CH), CH)
-            for f in range(2):
+            for f in fields:
                 body(f, rows)
             return carry
 
@@ -347,14 +355,6 @@
     tiles(3, first_x)
     chunks(first_y)
 
-    def send_data(k, carry):
-        route(sm, rm, k, s_m, r_m).wait_send()
-        route(sw, rw, k, s_w, r_w).wait_send()
-        route(sd, rd, k, s_d, r_d).start()
-        return carry
-
-    lax.fori_loop(1, NPY, send_data, 0)
-
     pick = jnp.where(iota((8, L), 0) < 3, 1.0, 0.0).astype(bf16)
     target = iota((T, 4 * CAP), 0).astype(f32)
 
@@ -371,9 +371,13 @@
             rows = slice(i * CAP, (i + 1) * CAP)
             if with_meta:
                 meta = rm[k]
-                s = lax.dot_general(meta.astype(bf16), pick, TN, preferred_element_type=f32)
+                s = meta[0:1, :]
+                hi = s.astype(bf16).astype(f32)
+                mid = (s - hi).astype(bf16).astype(f32)
+                three = jnp.concatenate([hi, mid, s - hi - mid, jnp.zeros((5, CAP), f32)], axis=0)
+                s = lax.dot_general(three.astype(bf16), pick, TN, preferred_element_type=f32)
                 shares_of[k] = s
-                tid[0:1, rows] = meta[4:5, :] * 32.0 + meta[3:4, :]
+                tid[0:1, rows] = meta[1:2, :]
             else:
                 s = shares_of[k]
             v = land[k]
@@ -417,10 +421,35 @@
 
     lax.fori_loop(0, 4, d_group, 0)
     bfield[0] = (column(0) + pltpu.roll(column(1), 1, 0)).reshape(NB, 2, 16, L)
-    pack(bfield, bsend)
-    start_turn(bsend, bext, s_b, r_b)
+
+    def b_pack(f, p):
+        right = bfield[0, lax.rem(2 * p + 2, NB), f]
+        left = bfield[0, lax.rem(2 * p + NB - 1, NB), f]
+        return [bfield[0, 2 * p, f], bfield[0, 2 * p + 1, f], jnp.where(lanes16 < 64, right, left)]
+
+    def b_copy(f, k, source):
+        return pltpu.make_async_remote_copy(
+            src_ref=bsend.at[f, ypeer(k)],
+            dst_ref=bext.at[f, :, pl.ds(pl.multiple_of(source * 16, 16), 16), :],
+            send_sem=s_b.at[f, k], recv_sem=r_b.at[f, k],
+            device_id={"px": ypeer(k)}, device_id_type=MESH,
+        )
+
+    for f in range(2):
+        def b_send(k, carry, f=f):
+            for j, tile in enumerate(b_pack(f, ypeer(k))):
+                bsend[f, ypeer(k), j] = tile
+            b_copy(f, k, px).start()
+            return carry
+
+        lax.fori_loop(1, NPX, b_send, 0)
+    for f in range(2):
+        for j, tile in enumerate(b_pack(f, px)):
+            bext[f, j, pl.ds(pl.multiple_of(px * 16, 16), 16), :] = tile
 
     def drain_py(k, carry):
+        route(sm, rm, k, s_m, r_m).wait_send()
+        route(sw, rw, k, s_w, r_w).wait_send()
         route(sd, rd, k, s_d, r_d).wait_send()
         return carry
 
@@ -446,7 +475,6 @@
     tiles(3, image_start)
     lax.fori_loop(1, NPY, drain_py, 0)
     free_turn(tsend, text, s_t, r_t)
-    end_turn(bsend, bext, s_b, r_b)
 
     dots[...] = jnp.zeros_like(dots)
 
@@ -454,23 +482,20 @@
         dots[n] += jnp.sum((a * b).reshape(-1, 8, L), axis=0)
 
     def b_chunk(f, rows):
-        v = sweep_y([bext[0, j, f, rows, :] for j in range(3)], rows)
+        v = sweep_y([bext[f, j, rows, :] for j in range(3)], rows)
         for j in range(3):
             gbuf[j, f, rows, :] = v[j]
 
-    chunks(b_chunk)
 
     def residual_tile(j, f):
         r = sweep_x(gbuf[j, f], j) - abuf[j, f]
         rbuf[j, f] = r
 
-        @pl.when(j < 2)
-        def _():
+        if j < 2:
             add_dot(0, r, r)
 
         ubuf[j, f] = sweep_x(r, j)
 
-    tiles(3, residual_tile)
 
     def q_chunk(f, rows):
         u = sweep_y([ubuf[j, f, rows, :] for j in range(3)], rows)
@@ -481,19 +506,16 @@
         for j in range(3):
             gbuf[j, f, rows, :] = v[j]
 
-    chunks(q_chunk)
 
     def q_tile(j, f):
         q = rbuf[j, f] + sweep_x(gbuf[j, f], j)
         qbuf[j, f] = q
 
-        @pl.when(j < 2)
-        def _():
+        if j < 2:
             add_dot(2, q, q)
 
         ubuf[j, f] = sweep_x(q, j)
 
-    tiles(3, q_tile)
 
     def p_up(f, rows):
         u = sweep_y([ubuf[j, f, rows, :] for j in range(3)], rows)
@@ -503,7 +525,17 @@
         for j in range(3):
             ubuf[j, f, rows, :] = v[j]
 
-    chunks(p_up)
+    for f in range(2):
+        def b_wait(k, carry, f=f):
+            b_copy(f, k, lax.rem(px + NPX - k, NPX)).wait_recv()
+            return carry
+
+        lax.fori_loop(1, NPX, b_wait, 0)
+        chunks(b_chunk, (f,))
+        tiles(3, residual_tile, (f,))
+        chunks(q_chunk, (f,))
+        tiles(3, q_tile, (f,))
+        chunks(p_up, (f,))
 
     def p_down(f, rows):
         v = sweep_y([ubuf[j, f, rows, :] for j in range(3)], rows, 2)
@@ -527,6 +559,12 @@
             src_ref=red2.at[0], dst_ref=red2.at[k], send_sem=s_2.at[k], recv_sem=r_2.at[k],
             device_id={"py": opeer(k)}, device_id_type=MESH,
         )
+
+    def put(n, buf, out):
+        return [
+            pltpu.make_async_copy(buf.at[j], out.at[:, :, j * L:(j + 1) * L], s_o.at[2 * n + j])
+            for j in range(2)
+        ]
 
     def merge(count, send, buf):
         for k in range(1, count):
@@ -538,14 +576,25 @@
 
     for k in range(1, NPX):
         sum1(k).start()
+    outs = put(0, rbuf, o_r) + put(1, qbuf, o_q)
+    for copy in outs:
+        copy.start()
     chunks(p_down)
-    free_turn(bsend, bext, s_b, r_b)
+    for f in range(2):
+        def b_free(k, carry, f=f):
+            b_copy(f, k, px).wait_send()
+            return carry
+
+        lax.fori_loop(1, NPX, b_free, 0)
     red2[0] = merge(NPX, sum1, red1)
     for k in range(1, NPY):
         sum2(k).start()
     for k in range(1, NPX):
         sum1(k).wait_send()
     tiles(2, p_tile)
+    last = put(2, abuf, o_p)
+    for copy in last:
+        copy.start()
     total = merge(NPY, sum2, red2)
     sums = jnp.sum(total, axis=1, keepdims=True)
     rr, gain, qq, gain2 = [sums[n:n + 1, :] for n in range(4)]
@@ -559,15 +608,20 @@
     kr = alpha + alpha2 * grow
     kq = -alpha2 * alpha
 
-    for j in range(2):
-        for f in range(2):
-            r = rbuf[j, f]
-            q = qbuf[j, f]
-            ctl[f, :, j * L:(j + 1) * L] = cc[j, f] + kr * r + kq * q
-            res[f, :, j * L:(j + 1) * L] = r - kr * q - kq * abuf[j, f]
-
+    o_k[0:1, :] = jnp.broadcast_to(kr, (1, L))
+    o_k[1:2, :] = jnp.broadcast_to(kq, (1, L))
+    for copy in outs + last:
+        copy.wait()
     for k in range(1, NPY):
         sum2(k).wait_send()
+
+
+def finish(c, r, q, p, k, control, residual):
+    kr = k[0:1, 0:1]
+    kq = k[1:2, 0:1]
+    for f in range(2):
+        control[f] = c[f] + kr * r[f] + kq * q[f]
+        residual[f] = r[f] - kr * q[f] - kq * p[f]
 
 
 def shards(control_start, coef_x, coef_y, innovation, obs_weight, interp, obs_owner, cell_key, stencil):
@@ -579,27 +633,27 @@
         vm((ROWS, L), f32), vm((ROWS, L), f32), vm((16, NB * L), f32), dma((11,)),
         vm((2 * M + 1, 3, L, L), f32), vm((2 * M + 1, 3, L, L), f32),
         vm((L, L), f32), vm((ROWS, 4 * L), bf16), vm((8, ROWS), bf16), vm((CAP, ROWS), bf16),
-        vm((NPY, CAP, L), f32), vm((NPY, CAP, L), f32), vm((NPY, 8, CAP), f32),
-        vm((NPY, CAP, L), f32), vm((NPY, CAP, L), f32), vm((NPY, 8, CAP), f32),
+        vm((NPY, CAP, L), f32), vm((NPY, CAP, L), f32), vm((NPY, 2, CAP), f32),
+        vm((NPY, CAP, L), f32), vm((NPY, CAP, L), f32), vm((NPY, 2, CAP), f32),
         vm((4 * CAP, 6 * L), bf16), vm((8, 4 * CAP), f32), vm((T, 6 * L), f32),
         vm((2, NB, 2, 16, L), f32), vm((NPX, 2, 3, 2, 16, L), f32),
-        vm((1, NB, 2, 16, L), f32), vm((NPX, 1, 3, 2, 16, L), f32),
+        vm((1, NB, 2, 16, L), f32), vm((2, NPX, 3, 16, L), f32),
         vm((1, NB, 1, 16, L), f32), vm((NPX, 1, 3, 1, 16, L), f32),
         vm((3, 3, L, L), f32), vm((2, 3, L, L), f32),
-        vm((2, 3, 2, L, L), f32), vm((1, 3, 2, L, L), f32), vm((1, 3, 1, L, L), f32),
+        vm((2, 3, 2, L, L), f32), vm((2, 3, L, L), f32), vm((1, 3, 1, L, L), f32),
         field, field, field, field, field,
         vm((4, 8, L), f32), vm((NPX, 8, L), f32), vm((NPY, 8, L), f32),
         vm((4, T, 4 * CAP), bf16), vm((NPY, CAP, L), f32),
         dma((NPY,)), dma((NPY,)), dma((NPY,)), dma((NPY,)), dma((NPY,)), dma((NPY,)),
-        dma((NPX,)), dma((NPX,)), dma((NPX,)), dma((NPX,)), dma((NPX,)), dma((NPX,)),
-        dma((2,)), dma((2,)), dma((NPX,)), dma((NPX,)), dma((NPY,)), dma((NPY,)),
+        dma((NPX,)), dma((NPX,)), dma((2, NPX)), dma((2, NPX)), dma((NPX,)), dma((NPX,)),
+        dma((2,)), dma((2,)), dma((NPX,)), dma((NPX,)), dma((NPY,)), dma((NPY,)), dma((6,)),
     ]
     out = jax.ShapeDtypeStruct((2, L, 2 * L), f32)
-    control, residual = pl.pallas_call(
+    r, q, p, k = pl.pallas_call(
         kernel,
-        out_shape=(out, out),
+        out_shape=(out, out, out, jax.ShapeDtypeStruct((2, L), f32)),
         in_specs=[pl.BlockSpec(memory_space=pltpu.HBM)] * 9,
-        out_specs=(pl.BlockSpec(memory_space=pltpu.VMEM),) * 2,
+        out_specs=(pl.BlockSpec(memory_space=pltpu.HBM),) * 3 + (pl.BlockSpec(memory_space=pltpu.VMEM),),
         scratch_shapes=scratch,
         compiler_params=pltpu.CompilerParams(
             collective_id=0, has_side_effects=True, vmem_limit_bytes=60 * 1024 * 1024
@@ -611,6 +665,11 @@
         coef_y.reshape(16, NB * L),
     )
     shape = control_start.shape
+    control, residual = pl.pallas_call(
+        finish, out_shape=(out, out), name="finish",
+        in_specs=[pl.BlockSpec(memory_space=pltpu.VMEM)] * 5,
+        compiler_params=pltpu.CompilerParams(vmem_limit_bytes=60 * 1024 * 1024),
+    )(control_start.reshape(2, L, 2 * L), r, q, p, k)
     return control.reshape(shape), residual.reshape(shape)
 
 

time: 75.8 us -> 73.2 us (0.966)
  local copies, waits for them, and re-layouts: 2.42 us -> 0 us
    unnamed x4 -> x0, local copies, waits for them, and re-layouts: 2.42 us -> none
    pallas_call x1 -> x2, Pallas kernels: 72.6 us -> 72.4 us  [the longest x1 70.3 us: shards(): pl.pallas_call(kernel, out_shape=(out, out, out, jax.ShapeDtypeStruct((2,...]
where the time goes in v5:
time: 73.2 us; the launch traced here: 73 us
  Pallas kernels  72.4 us (99%)
    pallas_call x1, Pallas kernels, shards(): pl.pallas_call(kernel, out_shape=(out, out, out, jax.ShapeDtypeStruct((2,...  70.3 us
    pallas_call x1, Pallas kernels, shards(): pl.pallas_call(finish, out_shape=(out, out), name='finish', in_specs=[pl....  2.1 us

profile of v5, /device:TPU:1, one launch (start us, length us, event | category | flops | bytes accessed | tf_op | source)
XLA Modules:
  0.0 73.0 jit_solution(12954718471848895223)
XLA Ops:
  0.6 70.3 %assimilate.1 = (f32[2,128,256]{2,1,0:T(8,128)}, f32[2,128,256]{2,1,0:T(8,128)}, f32[2,128,256]{2,1,0:T(8,128)}, f32[2,128]{1,0:T(2,128)}) custom-call(s32[8,128]{1,0:T(8,128)} %bitcast.17, s32[8,128]{1,0:T(8,128)} %bitcast.18, s32[8,128]{1,0:T(8,128)} %bitcast.19, f32[8,128]{1,0:T(8,128)} %bitcast.20, f32[1024,128]{1,0:T(8,128)} %h_inn.1, ...), custom_call_target="tpu_custom_call" | custom-call | tf_op jit(solution)/shard_map/assimilate/pallas_call | solution.py:652
  70.9 2.1 %finish.1 = (f32[2,128,256]{2,1,0:T(8,128)}, f32[2,128,256]{2,1,0:T(8,128)}) custom-call(f32[2,128,256]{2,1,0:T(8,128)} %bitcast.14, f32[2,128,256]{2,1,0:T(8,128)} %get-tuple-element.8.r, f32[2,128,256]{2,1,0:T(8,128)} %get-tuple-element.9.q, f32[2,128,256]{2,1,0:T(8,128)} %get-tuple-element.10.p, f32[2,128]{1,0:T(2,128)} %get-tuple-element.11.k), custom_call_target="tpu_custom_call" | custom-call | tf_op jit(solution)/shard_map/finish/pallas_call | solution.py:668

commit v6 on v5

--- a/solution.py
+++ b/solution.py
@@ -220,7 +220,6 @@
 
         lax.fori_loop(1, NPX, one, 0)
 
-    pl.semaphore_wait(barrier, NPX - 1 + NPY - 1)
 
     def edge(side):
         peer = ypeer(1 if side == 1 else NPX - 1)
@@ -249,6 +248,23 @@
         out = dot(pbuf[...], vals[...])
         return meta, out[:, 0:L] + out[:, L:2 * L], out[:, 2 * L:3 * L] + out[:, 3 * L:4 * L]
 
+    def fill_rows(k, carry):
+        meta, w, wd = gather(k)
+        sm[k] = meta
+        sw[k] = w
+        sd[k] = wd
+        return carry
+
+    lax.fori_loop(1, 6, fill_rows, 0)
+    pl.semaphore_wait(barrier, NPX - 1 + NPY - 1)
+
+    def start_rows(k, carry):
+        route(sm, rm, k, s_m, r_m).start()
+        route(sw, rw, k, s_w, r_w).start()
+        return carry
+
+    lax.fori_loop(1, 6, start_rows, 0)
+
     def send_rows(k, carry):
         meta, w, wd = gather(k)
         sm[k] = meta
@@ -258,7 +274,7 @@
         route(sw, rw, k, s_w, r_w).start()
         return carry
 
-    lax.fori_loop(1, NPY, send_rows, 0)
+    lax.fori_loop(6, NPY, send_rows, 0)
 
     def send_data(k, carry):
         route(sd, rd, k, s_d, r_d).start()
@@ -442,7 +458,8 @@
             b_copy(f, k, px).start()
             return carry
 
-        lax.fori_loop(1, NPX, b_send, 0)
+        for k in (4, 3, 5, 2, 6, 1, 7):
+            b_send(k, 0)
     for f in range(2):
         for j, tile in enumerate(b_pack(f, px)):
             bext[f, j, pl.ds(pl.multiple_of(px * 16, 16), 16), :] = tile

time: 73.2 us -> 72.6 us (level)
  no operation moved by 1% of the time
where the time goes in v6:
time: 72.6 us; the launch traced here: 72.4 us
  Pallas kernels  71.8 us (99%)
    pallas_call x1, Pallas kernels, shards(): pl.pallas_call(kernel, out_shape=(out, out, out, jax.ShapeDtypeStruct((2,...  69.7 us
    pallas_call x1, Pallas kernels, shards(): pl.pallas_call(finish, out_shape=(out, out), name='finish', in_specs=[pl....  2.1 us

profile of v6, /device:TPU:1, one launch (start us, length us, event | category | flops | bytes accessed | tf_op | source)
XLA Modules:
  0.0 72.4 jit_solution(4614897713751468501)
XLA Ops:
  0.6 69.7 %assimilate.1 = (f32[2,128,256]{2,1,0:T(8,128)}, f32[2,128,256]{2,1,0:T(8,128)}, f32[2,128,256]{2,1,0:T(8,128)}, f32[2,128]{1,0:T(2,128)}) custom-call(s32[8,128]{1,0:T(8,128)} %bitcast.17, s32[8,128]{1,0:T(8,128)} %bitcast.18, s32[8,128]{1,0:T(8,128)} %bitcast.19, f32[8,128]{1,0:T(8,128)} %bitcast.20, f32[1024,128]{1,0:T(8,128)} %h_inn.1, ...), custom_call_target="tpu_custom_call" | custom-call | tf_op jit(solution)/shard_map/assimilate/pallas_call | solution.py:669
  70.3 2.1 %finish.1 = (f32[2,128,256]{2,1,0:T(8,128)}, f32[2,128,256]{2,1,0:T(8,128)}) custom-call(f32[2,128,256]{2,1,0:T(8,128)} %bitcast.14, f32[2,128,256]{2,1,0:T(8,128)} %get-tuple-element.8.r, f32[2,128,256]{2,1,0:T(8,128)} %get-tuple-element.9.q, f32[2,128,256]{2,1,0:T(8,128)} %get-tuple-element.10.p, f32[2,128]{1,0:T(2,128)} %get-tuple-element.11.k), custom_call_target="tpu_custom_call" | custom-call | tf_op jit(solution)/shard_map/finish/pallas_call | solution.py:685

commit v7 on v6

--- a/solution.py
+++ b/solution.py
@@ -470,9 +470,6 @@
         route(sd, rd, k, s_d, r_d).wait_send()
         return carry
 
-    for side in range(2):
-        edge(side).wait_send()
-    free_turn(cysend, cyx, s_c, r_c)
     end_turn(tsend, text, s_t, r_t)
 
     def spread(f, rows, keep=3):
@@ -490,8 +487,6 @@
         abuf[j, f] = cc[j, f] + sweep_x(gbuf[j, f], j)
 
     tiles(3, image_start)
-    lax.fori_loop(1, NPY, drain_py, 0)
-    free_turn(tsend, text, s_t, r_t)
 
     dots[...] = jnp.zeros_like(dots)
 
@@ -609,6 +604,11 @@
     for k in range(1, NPX):
         sum1(k).wait_send()
     tiles(2, p_tile)
+    for side in range(2):
+        edge(side).wait_send()
+    free_turn(cysend, cyx, s_c, r_c)
+    free_turn(tsend, text, s_t, r_t)
+    lax.fori_loop(1, NPY, drain_py, 0)
     last = put(2, abuf, o_p)
     for copy in last:
         copy.start()

time: 72.6 us -> 72.6 us (level)
  no operation moved by 1% of the time
where the time goes in v7:
time: 72.6 us; the launch traced here: 72.4 us
  Pallas kernels  71.8 us (99%)
    pallas_call x1, Pallas kernels, shards(): pl.pallas_call(kernel, out_shape=(out, out, out, jax.ShapeDtypeStruct((2,...  69.7 us
    pallas_call x1, Pallas kernels, shards(): pl.pallas_call(finish, out_shape=(out, out), name='finish', in_specs=[pl....  2.1 us

profile of v7, /device:TPU:1, one launch (start us, length us, event | category | flops | bytes accessed | tf_op | source)
XLA Modules:
  0.0 72.4 jit_solution(4678942197207202419)
XLA Ops:
  0.6 69.7 %assimilate.1 = (f32[2,128,256]{2,1,0:T(8,128)}, f32[2,128,256]{2,1,0:T(8,128)}, f32[2,128,256]{2,1,0:T(8,128)}, f32[2,128]{1,0:T(2,128)}) custom-call(s32[8,128]{1,0:T(8,128)} %bitcast.17, s32[8,128]{1,0:T(8,128)} %bitcast.18, s32[8,128]{1,0:T(8,128)} %bitcast.19, f32[8,128]{1,0:T(8,128)} %bitcast.20, f32[1024,128]{1,0:T(8,128)} %h_inn.1, ...), custom_call_target="tpu_custom_call" | custom-call | tf_op jit(solution)/shard_map/assimilate/pallas_call | solution.py:669
  70.3 2.1 %finish.1 = (f32[2,128,256]{2,1,0:T(8,128)}, f32[2,128,256]{2,1,0:T(8,128)}) custom-call(f32[2,128,256]{2,1,0:T(8,128)} %bitcast.14, f32[2,128,256]{2,1,0:T(8,128)} %get-tuple-element.8.r, f32[2,128,256]{2,1,0:T(8,128)} %get-tuple-element.9.q, f32[2,128,256]{2,1,0:T(8,128)} %get-tuple-element.10.p, f32[2,128]{1,0:T(2,128)} %get-tuple-element.11.k), custom_call_target="tpu_custom_call" | custom-call | tf_op jit(solution)/shard_map/finish/pallas_call | solution.py:685
